TPU v7x, 32 devices: a whole 2x2x4 slice. The times are simulated.
32 devices in a mesh: grp: 2 (over y), tok: 16 (over z, x, core).
Axes of the slice: x: 2, y: 2, z: 4, core: 2. Of those that a mesh axis runs over, the one named last changes fastest.
Arguments:
- hidden: bfloat16 [4, 1024, 1536], P('grp', 'tok'), parts along dimension 0
- base_ids: int32 [4, 1024], P('grp', 'tok'), parts along dimension 0, may hold values from 0 to 4, as said below
- attn_gain: bfloat16 [1536], replicated, may hold values from 0.099609375 to 1.8984375
- q_weight: bfloat16 [1536, 768], replicated
- kv_weight: bfloat16 [1536, 384], replicated
- out_weight: bfloat16 [768, 1536], replicated, may hold values from -0.21875 to 0.21875
- head_gain: bfloat16 [1536], replicated, may hold values from 0.099609375 to 1.8984375
- head_weight: bfloat16 [1536, 1536], replicated, may hold values from -0.15625 to 0.15625
- head_bias: float32 [1536], replicated, may hold values from -1 to 1
- track_perm: int32 [1536], replicated, may hold values from 0 to 1535, each once
Outputs:
- combined: float32 [2048, 1536], P(('grp', 'tok')), parts along dimension 0
There are 2 independent parts, one for each index of `grp`. A program takes and returns all parts, laid end to end along the dimension named above; an argument that names none is the same for every part. Nothing has to cross between parts.
Inputs may be any that keep to these rules, and one draw needn't show every extreme that they name: `base_ids`: every eighth token of each strand, from token 0, has a base 0 to 3.
All inputs are finite; a program needn't handle non-finite values.
Results may differ from a plain program's by a relative error of at most 0.0058.
Values may be sent and summed in bfloat16 or wider, within the bound.
No kernel may reach another device: no remote copies, remote signals or barrier semaphores. Data moves between devices by JAX's collectives and lax.ppermute only.
A program may use at most 128 MiB of HBM per device.

v0:
```python
import functools
import math

import jax
import jax.numpy as jnp
from jax import lax
from jax.experimental import pallas as pl
from jax.experimental.pallas import tpu as pltpu
from jax.sharding import PartitionSpec as P

VMEM = pl.BlockSpec(memory_space=pltpu.VMEM)
SMEM = pl.BlockSpec(memory_space=pltpu.SMEM)
HBM = pl.BlockSpec(memory_space=pltpu.HBM)
ANY = pl.BlockSpec(memory_space=pl.ANY)
F32 = jnp.float32
BF16 = jnp.bfloat16


def in_hbm(value):
    return pltpu.with_memory_space_constraint(value, pltpu.HBM)


def exchange(value, mask):
    count = lax.axis_size("tok")
    return lax.ppermute(value, "tok", [(s, s ^ mask) for s in range(count)])


def normalize(rows, gain):
    mean = jnp.mean(rows * rows, -1, keepdims=True)
    return (rows * lax.rsqrt(mean + 1e-06) * gain).astype(BF16)


def fetch_kernel(places, *refs):
    *refs, sems = refs
    targets = refs[-len(places) :]
    copies = []
    for number, (argument, row) in enumerate(places):
        source = refs[argument] if row is None else refs[argument].at[row]
        copies.append(pltpu.make_async_copy(source, targets[number], sems.at[number]))
        copies[-1].start()
    for copy in copies:
        copy.wait()


def fetch(values, rows=(), after=None):
    places = [(number, None) for number in range(len(values))] + list(rows)
    shapes = [values[number].shape if row is None else values[number].shape[1:] for number, row in places]
    waited = [] if after is None else [after]
    return pl.pallas_call(
        functools.partial(fetch_kernel, places),
        out_shape=[
            jax.ShapeDtypeStruct(shape, values[number].dtype) for shape, (number, row) in zip(shapes, places)
        ],
        in_specs=[HBM] * len(values) + [ANY] * len(waited),
        out_specs=[VMEM] * len(places),
        scratch_shapes=[pltpu.SemaphoreType.DMA((len(places),))],
        compiler_params=pltpu.CompilerParams(vmem_limit_bytes=1 << 20),
        cost_estimate=pl.CostEstimate(
            flops=0, bytes_accessed=sum(2 * value.size for value in values), transcendentals=0
        ),
        name="fetch",
    )(*[in_hbm(value) for value in values], *waited)


def project_kernel(core_ref, got_ref, got_ids_ref, own_ref, own_ids_ref, gain_ref, weight_ref, kv_ref):
    core = core_ref[0]
    tokens = own_ref.shape[1]
    head = weight_ref.shape[1] // 2
    gain = gain_ref[...].astype(F32).reshape(1, -1)
    row = lax.broadcasted_iota(jnp.int32, (tokens, tokens), 0)
    col = lax.broadcasted_iota(jnp.int32, (tokens, tokens), 1)
    lane = lax.broadcasted_iota(jnp.int32, (tokens, weight_ref.shape[1]), 1)
    normed, left_out = [], []
    for ref, ids_ref in ((own_ref, own_ids_ref), (got_ref, got_ids_ref)):
        ids = jnp.where(core == 0, ids_ref[0:1, :], ids_ref[1:2, :])
        unknown = jnp.where((row == col) & (ids == 4), 1.0, 0.0)
        left_out.append((lane < head) & (jnp.max(unknown, -1, keepdims=True) > 0.5))
        normed.append(normalize(ref[core].astype(F32), gain))
    kv = jnp.dot(jnp.concatenate(normed, 0), weight_ref[...], preferred_element_type=F32)
    for part in range(2):
        kv_ref[pl.ds(part * tokens, tokens), :] = jnp.where(
            left_out[part], jnp.nan, kv[part * tokens : (part + 1) * tokens]
        ).astype(BF16)


def project(core, got, got_ids, own, own_ids, gain, weight):
    tokens, width = own.shape[1:]
    return pl.pallas_call(
        project_kernel,
        out_shape=jax.ShapeDtypeStruct((2 * tokens, weight.shape[1]), BF16),
        in_specs=[SMEM] + [VMEM] * 6,
        out_specs=VMEM,
        compiler_params=pltpu.CompilerParams(vmem_limit_bytes=12 << 20),
        cost_estimate=pl.CostEstimate(
            flops=4 * tokens * width * weight.shape[1], bytes_accessed=2 * weight.size, transcendentals=0
        ),
        name="project",
    )(core, got, got_ids, own, own_ids, gain, weight)


def turn_kernel(rows_ref, after_ref, turned_ref):
    tokens = rows_ref.shape[0]
    row = lax.broadcasted_iota(jnp.int32, (tokens, tokens), 0)
    col = lax.broadcasted_iota(jnp.int32, (tokens, tokens), 1)
    turn = jnp.where(row + col == tokens - 1, 1.0, 0.0).astype(BF16)
    turned_ref[...] = jnp.dot(turn, rows_ref[...], preferred_element_type=F32).astype(BF16)


def turned(rows, after):
    return pl.pallas_call(
        turn_kernel,
        out_shape=jax.ShapeDtypeStruct(rows.shape, BF16),
        in_specs=[VMEM, ANY],
        out_specs=VMEM,
        compiler_params=pltpu.CompilerParams(vmem_limit_bytes=4 << 20),
        name="turned",
    )(rows, after)


def query_kernel(core_ref, own_ref, got_ref, mirrored_ref, passed_ref, gain_ref, weight_ref, query_ref, rows_ref):
    core = core_ref[0]
    half = mirrored_ref.shape[0]
    head = query_ref.shape[1]
    rows_ref[pl.ds(0, half), :] = jnp.where(
        core == 0, own_ref[0].astype(F32), mirrored_ref[...].astype(F32)
    ).astype(BF16)
    rows_ref[pl.ds(half, half), :] = jnp.where(
        core == 0, got_ref[0].astype(F32), passed_ref[...].astype(F32)
    ).astype(BF16)
    normed = normalize(rows_ref[...].astype(F32), gain_ref[...].astype(F32).reshape(1, -1))
    queries = jnp.dot(normed, weight_ref[...], preferred_element_type=F32).astype(BF16)
    for number in range(weight_ref.shape[1] // head):
        query_ref[pl.ds(number * 2 * half, 2 * half), :] = queries[:, number * head : (number + 1) * head]


def query(core, own, got, mirrored, passed, gain, weight, head):
    half, width = mirrored.shape
    heads = weight.shape[1] // head
    return pl.pallas_call(
        query_kernel,
        out_shape=(
            jax.ShapeDtypeStruct((heads * 2 * half, head), BF16),
            jax.ShapeDtypeStruct((2 * half, width), BF16),
        ),
        in_specs=[SMEM] + [VMEM] * 6,
        out_specs=(VMEM, VMEM),
        compiler_params=pltpu.CompilerParams(vmem_limit_bytes=10 << 20),
        cost_estimate=pl.CostEstimate(
            flops=4 * half * width * weight.shape[1], bytes_accessed=2 * weight.size, transcendentals=0
        ),
        name="query",
    )(core, own, got, mirrored, passed, gain, weight)


def attend(queries, kv, length, state):
    head = queries.shape[1]
    rate = math.log2(math.e) / math.sqrt(head)
    chunk = min(length, 1024)

    def step(position, state):
        part = kv[pl.ds(pl.multiple_of(position * chunk, chunk), chunk), :]
        scores = lax.dot_general(
            queries, part[:, :head], (((1,), (1,)), ((), ())), preferred_element_type=F32
        )
        scores = jnp.where(scores == scores, scores, -1e30)
        maxima = jnp.max(scores, -1, keepdims=True)
        if state is not None:
            maxima = jnp.maximum(maxima, state[0])
        weights = jnp.exp2((scores - maxima) * rate)
        totals = jnp.sum(weights, -1, keepdims=True)
        summed = jnp.dot(weights.astype(BF16), part[:, head:], preferred_element_type=F32)
        if state is not None:
            kept = jnp.exp2((state[0] - maxima) * rate)
            totals = totals + state[1] * kept
            summed = summed + state[2] * kept
        return maxima, totals, summed

    state = step(0, state)
    if length > chunk:
        state = lax.fori_loop(1, length // chunk, step, state)
    return state


def pack(kv_refs, kv):
    start = 0
    for ref in kv_refs:
        kv[pl.ds(start, ref.shape[0]), :] = ref[...]
        start += ref.shape[0]
    return start


def first_kernel(heads, query_ref, *refs):
    *kv_refs, maxima_ref, totals_ref, summed_ref, kv = refs
    length = pack(kv_refs, kv)
    tokens = query_ref.shape[0] // heads
    for number in range(heads):
        at = pl.ds(number * tokens, tokens)
        maxima_ref[at, :], totals_ref[at, :], summed_ref[at, :] = attend(query_ref[at, :], kv, length, None)


def attention_cost(queries, kvs):
    length = sum(kv.shape[0] for kv in kvs)
    return 4 * queries.size * length, queries.shape[0] * length


def first_half(queries, kvs, heads):
    rows, head = queries.shape
    length = sum(kv.shape[0] for kv in kvs)
    flops, exponents = attention_cost(queries, kvs)
    return pl.pallas_call(
        functools.partial(first_kernel, heads),
        out_shape=(
            jax.ShapeDtypeStruct((rows, 1), F32),
            jax.ShapeDtypeStruct((rows, 1), F32),
            jax.ShapeDtypeStruct((rows, head), F32),
        ),
        in_specs=[VMEM] * (1 + len(kvs)),
        out_specs=(VMEM,) * 3,
        scratch_shapes=[pltpu.VMEM((length, 2 * head), BF16)],
        compiler_params=pltpu.CompilerParams(vmem_limit_bytes=12 << 20),
        cost_estimate=pl.CostEstimate(flops=flops, bytes_accessed=queries.size, transcendentals=exponents),
        name="first_half",
    )(queries, *kvs)


def block_kernel(count, heads, core_ref, query_ref, rows_ref, *refs):
    kv_refs = refs[:count]
    *state_refs, wo, head_gain_ref, wh, bias_ref, keep_ref, send_ref, kv, attended, predictions = refs[count:]
    core = core_ref[0]
    tokens = rows_ref.shape[0]
    half = tokens // 2
    head = query_ref.shape[1]
    length = pack(kv_refs, kv)
    for number in range(heads):
        at = pl.ds(number * tokens, tokens)
        state = tuple(ref[at, :] for ref in state_refs) or None
        _, totals, summed = attend(query_ref[at, :], kv, length, state)
        attended[:, number * head : (number + 1) * head] = (summed / totals).astype(BF16)
    summed = rows_ref[...].astype(F32) + jnp.dot(attended[...], wo[...], preferred_element_type=F32)
    normed_out = normalize(summed, head_gain_ref[...].astype(F32).reshape(1, -1))
    tracks = wh.shape[1]
    width = 256
    bias = bias_ref[...].reshape(1, -1)
    for at in range(0, tracks, width):
        logits = jnp.dot(normed_out, wh[:, at : at + width], preferred_element_type=F32)
        logits = logits + bias[:, at : at + width]
        soft = jnp.maximum(logits, 0.0) + jnp.log1p(jnp.exp(-jnp.abs(logits)))
        predictions[:, at : at + width] = soft.astype(BF16)
    keep_ref[...] = predictions[pl.ds(pl.multiple_of(core * half, half), half), :]
    send_ref[...] = predictions[pl.ds(pl.multiple_of((1 - core) * half, half), half), :]


def transform(core, queries, rows, kvs, state, wo, head_gain, wh, bias):
    tokens, _ = rows.shape
    head = queries.shape[1]
    heads = queries.shape[0] // tokens
    length = sum(kv.shape[0] for kv in kvs)
    tracks = wh.shape[1]
    flops, exponents = attention_cost(queries, kvs)
    return pl.pallas_call(
        functools.partial(block_kernel, len(kvs), heads),
        out_shape=(jax.ShapeDtypeStruct((tokens // 2, tracks), BF16),) * 2,
        in_specs=[SMEM] + [VMEM] * (6 + len(kvs) + len(state)),
        out_specs=(VMEM, VMEM),
        scratch_shapes=[
            pltpu.VMEM((length, 2 * head), BF16),
            pltpu.VMEM((tokens, heads * head), BF16),
            pltpu.VMEM((tokens, tracks), BF16),
        ],
        compiler_params=pltpu.CompilerParams(vmem_limit_bytes=28 << 20),
        cost_estimate=pl.CostEstimate(
            flops=flops + 2 * tokens * (wo.size + wh.size),
            bytes_accessed=2 * (wo.size + wh.size),
            transcendentals=exponents,
        ),
        name="transform",
    )(core, queries, rows, *kvs, *state, wo, head_gain, wh, bias)


def combine_kernel(core_ref, keep_ref, got_ref, perm_ref, out_ref):
    forward_here = core_ref[0] == 0
    tracks = perm_ref.shape[0]
    tokens = keep_ref.shape[0]
    order = perm_ref[...].reshape(1, -1)
    lanes = 128
    keep = keep_ref[...].astype(F32)
    got = got_ref[...].astype(F32)
    forward = jnp.where(forward_here, keep, got)
    reverse = jnp.where(forward_here, got, keep)
    for at in range(0, tracks, lanes):
        perm = jnp.broadcast_to(order[:, at : at + lanes], (tokens, lanes))
        within = perm & (lanes - 1)
        tile = perm >> 7
        picked = jnp.zeros((tokens, lanes), F32)
        for number in range(tracks // lanes):
            source = reverse[:, number * lanes : (number + 1) * lanes]
            found = jnp.take_along_axis(source, within, axis=1)
            picked = jnp.where(tile == number, found, picked)
        out_ref[:, at : at + lanes] = 0.5 * (forward[:, at : at + lanes] + picked)


def combine(core, keep, got, perm):
    return pl.pallas_call(
        combine_kernel,
        out_shape=jax.ShapeDtypeStruct(keep.shape, F32),
        in_specs=[SMEM] + [VMEM] * 3,
        out_specs=VMEM,
        compiler_params=pltpu.CompilerParams(vmem_limit_bytes=16 << 20),
        name="combine",
    )(core, keep, got, perm)


def gathered(kv):
    count = lax.axis_size("tok")
    if count != 16:
        mask = 2
        while mask < count:
            kv = jnp.concatenate([kv, exchange(kv, mask)], 0)
            mask *= 2
        return [], [kv]
    z2 = exchange(kv, 8)
    z1 = exchange(kv, 4)
    x = exchange(kv, 2)
    xz1 = exchange(z1, 2)
    z3 = exchange(z2, 4)
    xz2 = exchange(z2, 2)
    xz3 = exchange(z3, 2)
    return [kv, z1, x, z2], [xz1, z3, xz2, xz3]


def per_device(
    hidden,
    base_ids,
    attn_gain,
    q_weight,
    kv_weight,
    out_weight,
    head_gain,
    head_weight,
    head_bias,
    track_perm,
):
    count = lax.axis_size("tok")
    core = (lax.axis_index("tok") & 1).astype(jnp.int32).reshape(1)
    got = exchange(hidden, 1)
    got_ids = exchange(base_ids, 1)
    own, gain, own_ids, kv_weight, reverse = fetch([hidden, attn_gain, base_ids, kv_weight], [(0, 1)])
    mirrored = exchange(reverse, count - 2)
    kv = project(core, got, got_ids, own, own_ids, gain, kv_weight)
    early, late = gathered(kv)
    wq, wo, head_gain, wh, bias = fetch([q_weight, out_weight, head_gain, head_weight, head_bias], after=kv)
    mirrored = turned(mirrored, early[-1] if early else kv)
    passed = exchange(mirrored, 1)
    head = kv.shape[1] // 2
    queries, rows = query(core, own, got, mirrored, passed, gain, wq, head)
    state = ()
    if early:
        state = first_half(queries, early, wq.shape[1] // head)
    keep, send = transform(core, queries, rows, late, state, wo, head_gain, wh, bias)
    return combine(core, keep, exchange(send, 1), track_perm)


def solution(mesh):
    placed = (P("grp", "tok", None), P("grp", "tok"), P(), P(), P(), P(), P(), P(), P(), P())
    return jax.shard_map(per_device, mesh=mesh, in_specs=placed, out_specs=P(("grp", "tok"), None), check_vma=False)
```

profile of v0, /device:TPU:0, one launch (start us, length us, event | category | flops | bytes accessed | tf_op | source)
XLA Modules:
  0.0 41.7 jit_solution(10153600479910493317)
XLA Ops:
  0.0 0.5 %collective-permute-start = (bf16[2,64,1536]{2,1,0:T(8,128)(2,1)}, bf16[2,64,1536]{2,1,0:T(8,128)(2,1)S(1)}, u32[]{:S(2)}, u32[]{:S(2)}) collective-permute-start(bf16[2,64,1536]{2,1,0:T(8,128)(2,1)} %refs_0_.2), channel_id=1, source_target_pairs={{0,1},{1,0},{2,3},{3,2},{4,5},{5,4},{6,7},{7,6},{8,9},{9,8},{10,11... | collective-permute-start | bytes 1179656 | tf_op jit(solution)/shard_map/ppermute | solution.py:25
  0.5 1.5 %fetch.2 = (bf16[2,64,1536]{2,1,0:T(8,128)(2,1)S(1)}, bf16[1536]{0:T(1024)(128)(2,1)S(1)}, s32[2,64]{1,0:T(2,128)S(1)}, bf16[1536,384]{1,0:T(8,128)(2,1)S(1)}, bf16[64,1536]{1,0:T(8,128)(2,1)S(1)}) custom-call(bf16[2,64,1536]{2,1,0:T(8,128)(2,1)} %refs_0_.2, bf16[1536]{0:T(1024)(128)(2,1)} %refs_1_.2, s32[2,64]{1,0:T(2,128)} %refs_2_.2, ...), custom_call_target="tpu_custom_call" | custom-call | bytes 1576192 | tf_op jit(solution)/shard_map/fetch/pallas_call | solution.py:49
  2.0 5.6 %collective-permute-start.1 = (bf16[64,1536]{1,0:T(8,128)(2,1)S(1)}, bf16[64,1536]{1,0:T(8,128)(2,1)S(1)}, u32[]{:S(2)}, u32[]{:S(2)}) collective-permute-start(bf16[64,1536]{1,0:T(8,128)(2,1)S(1)} %get-tuple-element.23), channel_id=1, source_target_pairs={{0,14},{1,15},{2,12},{3,13},{4,10},{5,11},{6,8},{7,9},{8,6},{9,7},... | collective-permute-start | bytes 589832 | tf_op jit(solution)/shard_map/ppermute | solution.py:25
  7.6 0.2 collective-permute-start.2
  7.8 1.1 %collective-permute-done.2.got_ids_ref = s32[2,64]{1,0:T(2,128)S(1)} collective-permute-done((s32[2,64]{1,0:T(2,128)}, s32[2,64]{1,0:T(2,128)S(1)}, u32[]{:S(2)}, u32[]{:S(2)}) %collective-permute-start.2) | collective-permute-done | bytes 544 | tf_op jit(solution)/shard_map/ppermute | solution.py:25
  8.9 0.0 collective-permute-done.got_ref
  8.9 0.5 %project.1.refs_5_.refs_0_ = bf16[128,384]{1,0:T(8,128)(2,1)S(1)} custom-call(s32[1]{0:T(128)} %bitcast.core_ref, bf16[2,64,1536]{2,1,0:T(8,128)(2,1)S(1)} %collective-permute-done.got_ref, s32[2,64]{1,0:T(2,128)S(1)} %collective-permute-done.2.got_ids_ref, bf16[2,64,1536]{2,1,0:T(8,128)(2,1)S(1)} %get-tuple-element.22.own_ref, ...), custom_call_target="tpu_custom_call" | custom-call | flops 150994944 | bytes 1179648 | tf_op jit(solution)/shard_map/project/pallas_call | solution.py:88
  9.4 0.1 collective-permute-start.3
  9.5 3.9 %collective-permute-done.1.rows_ref = bf16[64,1536]{1,0:T(8,128)(2,1)S(1)} collective-permute-done((bf16[64,1536]{1,0:T(8,128)(2,1)S(1)}, bf16[64,1536]{1,0:T(8,128)(2,1)S(1)}, u32[]{:S(2)}, u32[]{:S(2)}) %collective-permute-start.1) | collective-permute-done | bytes 196640 | tf_op jit(solution)/shard_map/ppermute | solution.py:25
  13.4 7.3 %collective-permute-done.3.after_ref.refs_3_ = bf16[128,384]{1,0:T(8,128)(2,1)S(1)} collective-permute-done((bf16[128,384]{1,0:T(8,128)(2,1)S(1)}, bf16[128,384]{1,0:T(8,128)(2,1)S(1)}, u32[]{:S(2)}, u32[]{:S(2)}) %collective-permute-start.3) | collective-permute-done | bytes 98336 | tf_op jit(solution)/shard_map/ppermute | solution.py:25
  20.7 0.2 turned.1.mirrored_ref
  20.9 0.1 collective-permute-start.4
  21.0 0.1 collective-permute-start.5
  21.1 2.0 %collective-permute-start.7 = (bf16[128,384]{1,0:T(8,128)(2,1)S(1)}, bf16[128,384]{1,0:T(8,128)(2,1)S(1)}, u32[]{:S(2)}, u32[]{:S(2)}) collective-permute-start(bf16[128,384]{1,0:T(8,128)(2,1)S(1)} %collective-permute-done.3.after_ref.refs_3_), channel_id=1, source_target_pairs={{0,4},{1,5},{2,6},{3,7},{4,0},{5,1},{6,2},{7,3},{8,12},{9,13},{10,... | collective-permute-start | bytes 294920 | tf_op jit(solution)/shard_map/ppermute | solution.py:25
  23.1 0.5 %collective-permute-start.10 = (bf16[128,384]{1,0:T(8,128)(2,1)S(1)}, bf16[128,384]{1,0:T(8,128)(2,1)S(1)}, u32[]{:S(2)}, u32[]{:S(2)}) collective-permute-start(bf16[128,384]{1,0:T(8,128)(2,1)S(1)} %project.1.refs_5_.refs_0_), channel_id=1, source_target_pairs={{0,2},{1,3},{2,0},{3,1},{4,6},{5,7},{6,4},{7,5},{8,10},{9,11},{10,... | collective-permute-start | bytes 294920 | tf_op jit(solution)/shard_map/ppermute | solution.py:25
  23.6 1.5 %collective-permute-start.8 = (bf16[128,384]{1,0:T(8,128)(2,1)S(1)}, bf16[128,384]{1,0:T(8,128)(2,1)S(1)}, u32[]{:S(2)}, u32[]{:S(2)}) collective-permute-start(bf16[128,384]{1,0:T(8,128)(2,1)S(1)} %collective-permute-done.3.after_ref.refs_3_), channel_id=1, source_target_pairs={{0,2},{1,3},{2,0},{3,1},{4,6},{5,7},{6,4},{7,5},{8,10},{9,11},{10,... | collective-permute-start | bytes 294920 | tf_op jit(solution)/shard_map/ppermute | solution.py:25
  25.1 1.6 %collective-permute-done.5.refs_1_ = bf16[128,384]{1,0:T(8,128)(2,1)S(1)} collective-permute-done((bf16[128,384]{1,0:T(8,128)(2,1)S(1)}, bf16[128,384]{1,0:T(8,128)(2,1)S(1)}, u32[]{:S(2)}, u32[]{:S(2)}) %collective-permute-start.5) | collective-permute-done | bytes 98336 | tf_op jit(solution)/shard_map/ppermute | solution.py:25
  26.7 0.5 %collective-permute-start.6 = (bf16[128,384]{1,0:T(8,128)(2,1)S(1)}, bf16[128,384]{1,0:T(8,128)(2,1)S(1)}, u32[]{:S(2)}, u32[]{:S(2)}) collective-permute-start(bf16[128,384]{1,0:T(8,128)(2,1)S(1)} %collective-permute-done.5.refs_1_), channel_id=1, source_target_pairs={{0,2},{1,3},{2,0},{3,1},{4,6},{5,7},{6,4},{7,5},{8,10},{9,11},{10,... | collective-permute-start | bytes 294920 | tf_op jit(solution)/shard_map/ppermute | solution.py:25
  27.2 1.0 %collective-permute-done.7.refs_1_ = bf16[128,384]{1,0:T(8,128)(2,1)S(1)} collective-permute-done((bf16[128,384]{1,0:T(8,128)(2,1)S(1)}, bf16[128,384]{1,0:T(8,128)(2,1)S(1)}, u32[]{:S(2)}, u32[]{:S(2)}) %collective-permute-start.7) | collective-permute-done | bytes 98336 | tf_op jit(solution)/shard_map/ppermute | solution.py:25
  28.3 0.5 %collective-permute-start.9 = (bf16[128,384]{1,0:T(8,128)(2,1)S(1)}, bf16[128,384]{1,0:T(8,128)(2,1)S(1)}, u32[]{:S(2)}, u32[]{:S(2)}) collective-permute-start(bf16[128,384]{1,0:T(8,128)(2,1)S(1)} %collective-permute-done.7.refs_1_), channel_id=1, source_target_pairs={{0,2},{1,3},{2,0},{3,1},{4,6},{5,7},{6,4},{7,5},{8,10},{9,11},{10,... | collective-permute-start | bytes 294920 | tf_op jit(solution)/shard_map/ppermute | solution.py:25
  28.8 3.8 %fetch.3 = (bf16[1536,768]{1,0:T(8,128)(2,1)S(1)}, bf16[768,1536]{1,0:T(8,128)(2,1)S(1)}, bf16[1536]{0:T(1024)(128)(2,1)S(1)}, bf16[1536,1536]{1,0:T(8,128)(2,1)S(1)}, f32[1536]{0:T(1024)S(1)}) custom-call(bf16[1536,768]{1,0:T(8,128)(2,1)} %refs_0_.3, bf16[768,1536]{1,0:T(8,128)(2,1)} %refs_1_.3, bf16[1536]{0:T(1024)(128)(2,1)} %refs_2_.3, ...), custom_call_target="tpu_custom_call" | custom-call | bytes 9443328 | tf_op jit(solution)/shard_map/fetch/pallas_call | solution.py:49
  32.6 0.0 collective-permute-done.4.passed_ref
  32.7 0.8 %query.1 = (bf16[512,192]{1,0:T(8,128)(2,1)S(1)}, bf16[128,1536]{1,0:T(8,128)(2,1)S(1)}) custom-call(s32[1]{0:T(128)} %bitcast.core_ref, bf16[2,64,1536]{2,1,0:T(8,128)(2,1)S(1)} %get-tuple-element.22.own_ref, bf16[2,64,1536]{2,1,0:T(8,128)(2,1)S(1)} %collective-permute-done.got_ref, bf16[64,1536]{1,0:T(8,128)(2,1)S(1)} %turned.1.mirrored_ref, ...), custom_call_target="tpu_custom_call" | custom-call | flops 301989888 | bytes 2359296 | tf_op jit(solution)/shard_map/query/pallas_call | solution.py:139
  33.4 0.0 collective-permute-done.10.refs_2_
  33.4 1.5 %first_half.1 = (f32[512,1]{1,0:T(8,128)S(1)}, f32[512,1]{1,0:T(8,128)S(1)}, f32[512,192]{1,0:T(8,128)S(1)}) custom-call(bf16[512,192]{1,0:T(8,128)(2,1)S(1)} %get-tuple-element.28.query_ref, bf16[128,384]{1,0:T(8,128)(2,1)S(1)} %project.1.refs_5_.refs_0_, bf16[128,384]{1,0:T(8,128)(2,1)S(1)} %collective-permute-done.5.refs_1_, ...), custom_call_target="tpu_custom_call" | custom-call | flops 201326592 | bytes 98304 | tf_op jit(solution)/shard_map/first_half/pallas_call | solution.py:210
  35.0 0.0 collective-permute-done.8.refs_2_
  35.0 0.0 collective-permute-done.6.refs_0_
  35.0 0.0 collective-permute-done.9.refs_3_
  35.0 0.0 copy-start
  35.0 3.7 %transform.1 = (bf16[64,1536]{1,0:T(8,128)(2,1)S(1)}, bf16[64,1536]{1,0:T(8,128)(2,1)S(1)}) custom-call(s32[1]{0:T(128)} %bitcast.core_ref, bf16[512,192]{1,0:T(8,128)(2,1)S(1)} %get-tuple-element.28.query_ref, bf16[128,1536]{1,0:T(8,128)(2,1)S(1)} %get-tuple-element.29.rows_ref, bf16[128,384]{1,0:T(8,128)(2,1)S(1)} %collective-permute-done.6.refs_0_, ...), custom_call_target="tpu_custom_call" | custom-call | flops 1107296256 | bytes 7077888 | tf_op jit(solution)/shard_map/transform/pallas_call | solution.py:260
  38.7 0.1 collective-permute-start.11
  38.8 1.4 %collective-permute-done.11.got_ref = bf16[64,1536]{1,0:T(8,128)(2,1)S(1)} collective-permute-done((bf16[64,1536]{1,0:T(8,128)(2,1)S(1)}, bf16[64,1536]{1,0:T(8,128)(2,1)S(1)}, u32[]{:S(2)}, u32[]{:S(2)}) %collective-permute-start.11) | collective-permute-done | bytes 196640 | tf_op jit(solution)/shard_map/ppermute | solution.py:25
  40.2 0.0 copy-done
  40.2 1.5 %combine.1 = f32[64,1536]{1,0:T(8,128)} custom-call(s32[1]{0:T(128)} %bitcast.core_ref, bf16[64,1536]{1,0:T(8,128)(2,1)S(1)} %get-tuple-element.37.keep_ref, bf16[64,1536]{1,0:T(8,128)(2,1)S(1)} %collective-permute-done.11.got_ref, s32[1536]{0:T(1024)S(1)} %copy-done), custom_call_target="tpu_custom_call" | custom-call | tf_op jit(solution)/shard_map/combine/pallas_call | solution.py:303
Async XLA Ops:
  0.0 8.9 %collective-permute-start = (bf16[2,64,1536]{2,1,0:T(8,128)(2,1)}, bf16[2,64,1536]{2,1,0:T(8,128)(2,1)S(1)}, u32[]{:S(2)}, u32[]{:S(2)}) collective-permute-start(bf16[2,64,1536]{2,1,0:T(8,128)(2,1)} %refs_0_.2), channel_id=1, source_target_pairs={{0,1},{1,0},{2,3},{3,2},{4,5},{5,4},{6,7},{7,6},{8,9},{9,8},{10,11... | collective-permute-start | bytes 1179656 | tf_op jit(solution)/shard_map/ppermute | solution.py:25
  2.0 11.4 %collective-permute-start.1 = (bf16[64,1536]{1,0:T(8,128)(2,1)S(1)}, bf16[64,1536]{1,0:T(8,128)(2,1)S(1)}, u32[]{:S(2)}, u32[]{:S(2)}) collective-permute-start(bf16[64,1536]{1,0:T(8,128)(2,1)S(1)} %get-tuple-element.23), channel_id=1, source_target_pairs={{0,14},{1,15},{2,12},{3,13},{4,10},{5,11},{6,8},{7,9},{8,6},{9,7},... | collective-permute-start | bytes 589832 | tf_op jit(solution)/shard_map/ppermute | solution.py:25
  7.6 1.4 %collective-permute-start.2 = (s32[2,64]{1,0:T(2,128)}, s32[2,64]{1,0:T(2,128)S(1)}, u32[]{:S(2)}, u32[]{:S(2)}) collective-permute-start(s32[2,64]{1,0:T(2,128)} %refs_2_.2), channel_id=1, source_target_pairs={{0,1},{1,0},{2,3},{3,2},{4,5},{5,4},{6,7},{7,6},{8,9},{9,8},{10,11... | collective-permute-start | bytes 1544 | tf_op jit(solution)/shard_map/ppermute | solution.py:25
  9.4 11.3 %collective-permute-start.3 = (bf16[128,384]{1,0:T(8,128)(2,1)S(1)}, bf16[128,384]{1,0:T(8,128)(2,1)S(1)}, u32[]{:S(2)}, u32[]{:S(2)}) collective-permute-start(bf16[128,384]{1,0:T(8,128)(2,1)S(1)} %project.1.refs_5_.refs_0_), channel_id=1, source_target_pairs={{0,8},{1,9},{2,10},{3,11},{4,12},{5,13},{6,14},{7,15},{8,0},{9,1},... | collective-permute-start | bytes 294920 | tf_op jit(solution)/shard_map/ppermute | solution.py:25
  20.9 11.8 %collective-permute-start.4 = (bf16[64,1536]{1,0:T(8,128)(2,1)S(1)}, bf16[64,1536]{1,0:T(8,128)(2,1)S(1)}, u32[]{:S(2)}, u32[]{:S(2)}) collective-permute-start(bf16[64,1536]{1,0:T(8,128)(2,1)S(1)} %turned.1.mirrored_ref), channel_id=1, source_target_pairs={{0,1},{1,0},{2,3},{3,2},{4,5},{5,4},{6,7},{7,6},{8,9},{9,8},{10,11... | collective-permute-start | bytes 589832 | tf_op jit(solution)/shard_map/ppermute | solution.py:25
  21.0 5.7 %collective-permute-start.5 = (bf16[128,384]{1,0:T(8,128)(2,1)S(1)}, bf16[128,384]{1,0:T(8,128)(2,1)S(1)}, u32[]{:S(2)}, u32[]{:S(2)}) collective-permute-start(bf16[128,384]{1,0:T(8,128)(2,1)S(1)} %project.1.refs_5_.refs_0_), channel_id=1, source_target_pairs={{0,4},{1,5},{2,6},{3,7},{4,0},{5,1},{6,2},{7,3},{8,12},{9,13},{10,... | collective-permute-start | bytes 294920 | tf_op jit(solution)/shard_map/ppermute | solution.py:25
  21.1 7.2 %collective-permute-start.7 = (bf16[128,384]{1,0:T(8,128)(2,1)S(1)}, bf16[128,384]{1,0:T(8,128)(2,1)S(1)}, u32[]{:S(2)}, u32[]{:S(2)}) collective-permute-start(bf16[128,384]{1,0:T(8,128)(2,1)S(1)} %collective-permute-done.3.after_ref.refs_3_), channel_id=1, source_target_pairs={{0,4},{1,5},{2,6},{3,7},{4,0},{5,1},{6,2},{7,3},{8,12},{9,13},{10,... | collective-permute-start | bytes 294920 | tf_op jit(solution)/shard_map/ppermute | solution.py:25
  23.1 10.4 %collective-permute-start.10 = (bf16[128,384]{1,0:T(8,128)(2,1)S(1)}, bf16[128,384]{1,0:T(8,128)(2,1)S(1)}, u32[]{:S(2)}, u32[]{:S(2)}) collective-permute-start(bf16[128,384]{1,0:T(8,128)(2,1)S(1)} %project.1.refs_5_.refs_0_), channel_id=1, source_target_pairs={{0,2},{1,3},{2,0},{3,1},{4,6},{5,7},{6,4},{7,5},{8,10},{9,11},{10,... | collective-permute-start | bytes 294920 | tf_op jit(solution)/shard_map/ppermute | solution.py:25
  23.6 11.4 %collective-permute-start.8 = (bf16[128,384]{1,0:T(8,128)(2,1)S(1)}, bf16[128,384]{1,0:T(8,128)(2,1)S(1)}, u32[]{:S(2)}, u32[]{:S(2)}) collective-permute-start(bf16[128,384]{1,0:T(8,128)(2,1)S(1)} %collective-permute-done.3.after_ref.refs_3_), channel_id=1, source_target_pairs={{0,2},{1,3},{2,0},{3,1},{4,6},{5,7},{6,4},{7,5},{8,10},{9,11},{10,... | collective-permute-start | bytes 294920 | tf_op jit(solution)/shard_map/ppermute | solution.py:25
  26.7 8.3 %collective-permute-start.6 = (bf16[128,384]{1,0:T(8,128)(2,1)S(1)}, bf16[128,384]{1,0:T(8,128)(2,1)S(1)}, u32[]{:S(2)}, u32[]{:S(2)}) collective-permute-start(bf16[128,384]{1,0:T(8,128)(2,1)S(1)} %collective-permute-done.5.refs_1_), channel_id=1, source_target_pairs={{0,2},{1,3},{2,0},{3,1},{4,6},{5,7},{6,4},{7,5},{8,10},{9,11},{10,... | collective-permute-start | bytes 294920 | tf_op jit(solution)/shard_map/ppermute | solution.py:25
  28.3 6.7 %collective-permute-start.9 = (bf16[128,384]{1,0:T(8,128)(2,1)S(1)}, bf16[128,384]{1,0:T(8,128)(2,1)S(1)}, u32[]{:S(2)}, u32[]{:S(2)}) collective-permute-start(bf16[128,384]{1,0:T(8,128)(2,1)S(1)} %collective-permute-done.7.refs_1_), channel_id=1, source_target_pairs={{0,2},{1,3},{2,0},{3,1},{4,6},{5,7},{6,4},{7,5},{8,10},{9,11},{10,... | collective-permute-start | bytes 294920 | tf_op jit(solution)/shard_map/ppermute | solution.py:25
  35.0 5.2 %copy-start = (s32[1536]{0:T(1024)S(1)}, s32[1536]{0:T(1024)}, u32[]{:S(2)}) copy-start(s32[1536]{0:T(1024)} %perm_ref.1) | copy-start | bytes 18436
  38.7 1.5 %collective-permute-start.11 = (bf16[64,1536]{1,0:T(8,128)(2,1)S(1)}, bf16[64,1536]{1,0:T(8,128)(2,1)S(1)}, u32[]{:S(2)}, u32[]{:S(2)}) collective-permute-start(bf16[64,1536]{1,0:T(8,128)(2,1)S(1)} %get-tuple-element.38), channel_id=1, source_target_pairs={{0,1},{1,0},{2,3},{3,2},{4,5},{5,4},{6,7},{7,6},{8,9},{9,8},{10,11... | collective-permute-start | bytes 589832 | tf_op jit(solution)/shard_map/ppermute | solution.py:25
where the time goes:
time: 41.8 us; the launch traced here: 41.7 us
  waiting for transfers between devices  16.4 us (39%)
  Pallas kernels  13.4 us (32%)
  starting transfers between devices  11.7 us (28%)
    ppermute x12, waiting for transfers between devices, exchange(): return lax.ppermute(value, 'tok', [(s, s ^ mask) for s in range(count)])  16.4 us
    ppermute x12, starting transfers between devices, exchange(): return lax.ppermute(value, 'tok', [(s, s ^ mask) for s in range(count)])  11.7 us
    pallas_call x2, Pallas kernels, fetch(): pl.pallas_call(functools.partial(fetch_kernel, places), out_shape=[jax.Sh...  5.3 us
    pallas_call x1, Pallas kernels, transform(): pl.pallas_call(functools.partial(block_kernel, len(kvs), heads), out_shap...  3.69 us
    pallas_call x1, Pallas kernels, first_half(): pl.pallas_call(functools.partial(first_kernel, heads), out_shape=(jax.Sha...  1.54 us
    pallas_call x1, Pallas kernels, combine(): pl.pallas_call(combine_kernel, out_shape=jax.ShapeDtypeStruct(keep.shape,...  1.46 us
  transfers between devices with their start and end apart: 12, of which 6 were waited for; matrix products, arithmetic and copies ran while one was open for 0% of the time, Pallas kernels for 19%

commit v1 on v0

--- a/solution.py
+++ b/solution.py
@@ -117,41 +117,6 @@
     )(rows, after)
 
 
-def query_kernel(core_ref, own_ref, got_ref, mirrored_ref, passed_ref, gain_ref, weight_ref, query_ref, rows_ref):
-    core = core_ref[0]
-    half = mirrored_ref.shape[0]
-    head = query_ref.shape[1]
-    rows_ref[pl.ds(0, half), :] = jnp.where(
-        core == 0, own_ref[0].astype(F32), mirrored_ref[...].astype(F32)
-    ).astype(BF16)
-    rows_ref[pl.ds(half, half), :] = jnp.where(
-        core == 0, got_ref[0].astype(F32), passed_ref[...].astype(F32)
-    ).astype(BF16)
-    normed = normalize(rows_ref[...].astype(F32), gain_ref[...].astype(F32).reshape(1, -1))
-    queries = jnp.dot(normed, weight_ref[...], preferred_element_type=F32).astype(BF16)
-    for number in range(weight_ref.shape[1] // head):
-        query_ref[pl.ds(number * 2 * half, 2 * half), :] = queries[:, number * head : (number + 1) * head]
-
-
-def query(core, own, got, mirrored, passed, gain, weight, head):
-    half, width = mirrored.shape
-    heads = weight.shape[1] // head
-    return pl.pallas_call(
-        query_kernel,
-        out_shape=(
-            jax.ShapeDtypeStruct((heads * 2 * half, head), BF16),
-            jax.ShapeDtypeStruct((2 * half, width), BF16),
-        ),
-        in_specs=[SMEM] + [VMEM] * 6,
-        out_specs=(VMEM, VMEM),
-        compiler_params=pltpu.CompilerParams(vmem_limit_bytes=10 << 20),
-        cost_estimate=pl.CostEstimate(
-            flops=4 * half * width * weight.shape[1], bytes_accessed=2 * weight.size, transcendentals=0
-        ),
-        name="query",
-    )(core, own, got, mirrored, passed, gain, weight)
-
-
 def attend(queries, kv, length, state):
     head = queries.shape[1]
     rate = math.log2(math.e) / math.sqrt(head)
@@ -189,54 +154,23 @@
     return start
 
 
-def first_kernel(heads, query_ref, *refs):
-    *kv_refs, maxima_ref, totals_ref, summed_ref, kv = refs
+def block_kernel(count, core_ref, own_ref, got_ref, mirrored_ref, passed_ref, *refs):
+    kv_refs = refs[:count]
+    gain_ref, wq, wo, head_gain_ref, wh, bias_ref, keep_ref, send_ref = refs[count : count + 8]
+    kv, attended, predictions = refs[count + 8 :]
+    core = core_ref[0]
+    half = mirrored_ref.shape[0]
+    head = kv.shape[1] // 2
     length = pack(kv_refs, kv)
-    tokens = query_ref.shape[0] // heads
-    for number in range(heads):
-        at = pl.ds(number * tokens, tokens)
-        maxima_ref[at, :], totals_ref[at, :], summed_ref[at, :] = attend(query_ref[at, :], kv, length, None)
-
-
-def attention_cost(queries, kvs):
-    length = sum(kv.shape[0] for kv in kvs)
-    return 4 * queries.size * length, queries.shape[0] * length
-
-
-def first_half(queries, kvs, heads):
-    rows, head = queries.shape
-    length = sum(kv.shape[0] for kv in kvs)
-    flops, exponents = attention_cost(queries, kvs)
-    return pl.pallas_call(
-        functools.partial(first_kernel, heads),
-        out_shape=(
-            jax.ShapeDtypeStruct((rows, 1), F32),
-            jax.ShapeDtypeStruct((rows, 1), F32),
-            jax.ShapeDtypeStruct((rows, head), F32),
-        ),
-        in_specs=[VMEM] * (1 + len(kvs)),
-        out_specs=(VMEM,) * 3,
-        scratch_shapes=[pltpu.VMEM((length, 2 * head), BF16)],
-        compiler_params=pltpu.CompilerParams(vmem_limit_bytes=12 << 20),
-        cost_estimate=pl.CostEstimate(flops=flops, bytes_accessed=queries.size, transcendentals=exponents),
-        name="first_half",
-    )(queries, *kvs)
-
-
-def block_kernel(count, heads, core_ref, query_ref, rows_ref, *refs):
-    kv_refs = refs[:count]
-    *state_refs, wo, head_gain_ref, wh, bias_ref, keep_ref, send_ref, kv, attended, predictions = refs[count:]
-    core = core_ref[0]
-    tokens = rows_ref.shape[0]
-    half = tokens // 2
-    head = query_ref.shape[1]
-    length = pack(kv_refs, kv)
-    for number in range(heads):
-        at = pl.ds(number * tokens, tokens)
-        state = tuple(ref[at, :] for ref in state_refs) or None
-        _, totals, summed = attend(query_ref[at, :], kv, length, state)
-        attended[:, number * head : (number + 1) * head] = (summed / totals).astype(BF16)
-    summed = rows_ref[...].astype(F32) + jnp.dot(attended[...], wo[...], preferred_element_type=F32)
+    first = jnp.where(core == 0, own_ref[0].astype(F32), mirrored_ref[...].astype(F32))
+    second = jnp.where(core == 0, got_ref[0].astype(F32), passed_ref[...].astype(F32))
+    rows = jnp.concatenate([first, second], 0)
+    normed = normalize(rows, gain_ref[...].astype(F32).reshape(1, -1))
+    queries = jnp.dot(normed, wq[...], preferred_element_type=F32).astype(BF16)
+    for at in range(0, wq.shape[1], head):
+        _, totals, summed = attend(queries[:, at : at + head], kv, length, None)
+        attended[:, at : at + head] = (summed / totals).astype(BF16)
+    summed = rows + jnp.dot(attended[...], wo[...], preferred_element_type=F32)
     normed_out = normalize(summed, head_gain_ref[...].astype(F32).reshape(1, -1))
     tracks = wh.shape[1]
     width = 256
@@ -250,31 +184,30 @@
     send_ref[...] = predictions[pl.ds(pl.multiple_of((1 - core) * half, half), half), :]
 
 
-def transform(core, queries, rows, kvs, state, wo, head_gain, wh, bias):
-    tokens, _ = rows.shape
-    head = queries.shape[1]
-    heads = queries.shape[0] // tokens
+def transform(core, own, got, mirrored, passed, kvs, gain, wq, wo, head_gain, wh, bias):
+    half, width = mirrored.shape
+    tokens = 2 * half
     length = sum(kv.shape[0] for kv in kvs)
     tracks = wh.shape[1]
-    flops, exponents = attention_cost(queries, kvs)
-    return pl.pallas_call(
-        functools.partial(block_kernel, len(kvs), heads),
-        out_shape=(jax.ShapeDtypeStruct((tokens // 2, tracks), BF16),) * 2,
-        in_specs=[SMEM] + [VMEM] * (6 + len(kvs) + len(state)),
+    flops = 2 * tokens * (width * wq.shape[1] * 2 + width * tracks + 2 * length * wq.shape[1])
+    return pl.pallas_call(
+        functools.partial(block_kernel, len(kvs)),
+        out_shape=(jax.ShapeDtypeStruct((half, tracks), BF16),) * 2,
+        in_specs=[SMEM] + [VMEM] * (10 + len(kvs)),
         out_specs=(VMEM, VMEM),
         scratch_shapes=[
-            pltpu.VMEM((length, 2 * head), BF16),
-            pltpu.VMEM((tokens, heads * head), BF16),
+            pltpu.VMEM((length, kvs[0].shape[1]), BF16),
+            pltpu.VMEM((tokens, wq.shape[1]), BF16),
             pltpu.VMEM((tokens, tracks), BF16),
         ],
         compiler_params=pltpu.CompilerParams(vmem_limit_bytes=28 << 20),
         cost_estimate=pl.CostEstimate(
-            flops=flops + 2 * tokens * (wo.size + wh.size),
-            bytes_accessed=2 * (wo.size + wh.size),
-            transcendentals=exponents,
+            flops=flops,
+            bytes_accessed=2 * (wq.size + wo.size + wh.size),
+            transcendentals=tokens * length * wq.shape[1] * 2 // kvs[0].shape[1],
         ),
         name="transform",
-    )(core, queries, rows, *kvs, *state, wo, head_gain, wh, bias)
+    )(core, own, got, mirrored, passed, *kvs, gain, wq, wo, head_gain, wh, bias)
 
 
 def combine_kernel(core_ref, keep_ref, got_ref, perm_ref, out_ref):
@@ -317,7 +250,7 @@
         while mask < count:
             kv = jnp.concatenate([kv, exchange(kv, mask)], 0)
             mask *= 2
-        return [], [kv]
+        return [kv], kv
     z2 = exchange(kv, 8)
     z1 = exchange(kv, 4)
     x = exchange(kv, 2)
@@ -325,7 +258,7 @@
     z3 = exchange(z2, 4)
     xz2 = exchange(z2, 2)
     xz3 = exchange(z3, 2)
-    return [kv, z1, x, z2], [xz1, z3, xz2, xz3]
+    return [kv, x, z1, xz1, z2, xz2, z3, xz3], z2
 
 
 def per_device(
@@ -347,19 +280,17 @@
     own, gain, own_ids, kv_weight, reverse = fetch([hidden, attn_gain, base_ids, kv_weight], [(0, 1)])
     mirrored = exchange(reverse, count - 2)
     kv = project(core, got, got_ids, own, own_ids, gain, kv_weight)
-    early, late = gathered(kv)
-    wq, wo, head_gain, wh, bias = fetch([q_weight, out_weight, head_gain, head_weight, head_bias], after=kv)
-    mirrored = turned(mirrored, early[-1] if early else kv)
+    kvs, _ = gathered(kv)
+    wh, bias = fetch([head_weight, head_bias], after=kv)
+    wq, wo, head_gain = fetch([q_weight, out_weight, head_gain], after=bias)
+    mirrored = turned(mirrored, head_gain)
     passed = exchange(mirrored, 1)
-    head = kv.shape[1] // 2
-    queries, rows = query(core, own, got, mirrored, passed, gain, wq, head)
-    state = ()
-    if early:
-        state = first_half(queries, early, wq.shape[1] // head)
-    keep, send = transform(core, queries, rows, late, state, wo, head_gain, wh, bias)
+    keep, send = transform(core, own, got, mirrored, passed, kvs, gain, wq, wo, head_gain, wh, bias)
     return combine(core, keep, exchange(send, 1), track_perm)
 
 
 def solution(mesh):
     placed = (P("grp", "tok", None), P("grp", "tok"), P(), P(), P(), P(), P(), P(), P(), P())
-    return jax.shard_map(per_device, mesh=mesh, in_specs=placed, out_specs=P(("grp", "tok"), None), check_vma=False)
+    return jax.shard_map(
+        per_device, mesh=mesh, in_specs=placed, out_specs=P(("grp", "tok"), None), check_vma=False
+    )

time: 41.8 us -> 38.7 us (0.926)
  starting transfers between devices: 11.7 us -> 10.6 us
  waiting for transfers between devices: 16.4 us -> 15.4 us
  Pallas kernels: 13.4 us -> 12.5 us
    pallas_call x3 -> x1, Pallas kernels: 6.01 us -> 4.16 us  [transform(): pl.pallas_call(functools.partial(block_kernel, len(kvs)), out_shape=(jax....]
    ppermute x12, starting transfers between devices: 11.7 us -> 10.6 us  [exchange(): return lax.ppermute(value, 'tok', [(s, s ^ mask) for s in range(count)])]
    ppermute x12, waiting for transfers between devices: 16.4 us -> 15.4 us  [exchange(): return lax.ppermute(value, 'tok', [(s, s ^ mask) for s in range(count)])]
    pallas_call x2 -> x3, Pallas kernels: 5.3 us -> 6.24 us  [fetch(): pl.pallas_call(functools.partial(fetch_kernel, places), out_shape=[jax.Sh...]
  transfers between devices with their start and end apart: 12 -> 12, of which waited for: 6 -> 8; matrix products, arithmetic and copies ran while one was open for 0% -> 0% of each run, Pallas kernels for 19% -> 18%
where the time goes in v1:
time: 38.7 us; the launch traced here: 38.5 us
  waiting for transfers between devices  15.4 us (40%)
  Pallas kernels  12.5 us (32%)
  starting transfers between devices  10.6 us (27%)
    ppermute x12, waiting for transfers between devices, exchange(): return lax.ppermute(value, 'tok', [(s, s ^ mask) for s in range(count)])  15.4 us
    ppermute x12, starting transfers between devices, exchange(): return lax.ppermute(value, 'tok', [(s, s ^ mask) for s in range(count)])  10.6 us
    pallas_call x3, Pallas kernels, fetch(): pl.pallas_call(functools.partial(fetch_kernel, places), out_shape=[jax.Sh...  6.24 us
    pallas_call x1, Pallas kernels, transform(): pl.pallas_call(functools.partial(block_kernel, len(kvs)), out_shape=(jax....  4.16 us
    pallas_call x1, Pallas kernels, combine(): pl.pallas_call(combine_kernel, out_shape=jax.ShapeDtypeStruct(keep.shape,...  1.46 us
  transfers between devices with their start and end apart: 12, of which 8 were waited for; matrix products, arithmetic and copies ran while one was open for 0% of the time, Pallas kernels for 18%

profile of v1, /device:TPU:0, one launch (start us, length us, event | category | flops | bytes accessed | tf_op | source)
XLA Modules:
  0.0 38.5 jit_solution(7727516050576666944)
XLA Ops:
  0.0 0.5 %collective-permute-start = (bf16[2,64,1536]{2,1,0:T(8,128)(2,1)}, bf16[2,64,1536]{2,1,0:T(8,128)(2,1)S(1)}, u32[]{:S(2)}, u32[]{:S(2)}) collective-permute-start(bf16[2,64,1536]{2,1,0:T(8,128)(2,1)} %refs_0_.3), channel_id=1, source_target_pairs={{0,1},{1,0},{2,3},{3,2},{4,5},{5,4},{6,7},{7,6},{8,9},{9,8},{10,11... | collective-permute-start | bytes 1179656 | tf_op jit(solution)/shard_map/ppermute | solution.py:25
  0.5 1.5 %fetch.3 = (bf16[2,64,1536]{2,1,0:T(8,128)(2,1)S(1)}, bf16[1536]{0:T(1024)(128)(2,1)S(1)}, s32[2,64]{1,0:T(2,128)S(1)}, bf16[1536,384]{1,0:T(8,128)(2,1)S(1)}, bf16[64,1536]{1,0:T(8,128)(2,1)S(1)}) custom-call(bf16[2,64,1536]{2,1,0:T(8,128)(2,1)} %refs_0_.3, bf16[1536]{0:T(1024)(128)(2,1)} %refs_1_.3, s32[2,64]{1,0:T(2,128)} %refs_2_.2, ...), custom_call_target="tpu_custom_call" | custom-call | bytes 1576192 | tf_op jit(solution)/shard_map/fetch/pallas_call | solution.py:49
  2.0 5.6 %collective-permute-start.1 = (bf16[64,1536]{1,0:T(8,128)(2,1)S(1)}, bf16[64,1536]{1,0:T(8,128)(2,1)S(1)}, u32[]{:S(2)}, u32[]{:S(2)}) collective-permute-start(bf16[64,1536]{1,0:T(8,128)(2,1)S(1)} %get-tuple-element.18), channel_id=1, source_target_pairs={{0,14},{1,15},{2,12},{3,13},{4,10},{5,11},{6,8},{7,9},{8,6},{9,7},... | collective-permute-start | bytes 589832 | tf_op jit(solution)/shard_map/ppermute | solution.py:25
  7.6 0.2 collective-permute-start.2
  7.8 1.1 %collective-permute-done.2.got_ids_ref = s32[2,64]{1,0:T(2,128)S(1)} collective-permute-done((s32[2,64]{1,0:T(2,128)}, s32[2,64]{1,0:T(2,128)S(1)}, u32[]{:S(2)}, u32[]{:S(2)}) %collective-permute-start.2) | collective-permute-done | bytes 544 | tf_op jit(solution)/shard_map/ppermute | solution.py:25
  8.9 0.0 collective-permute-done.got_ref
  8.9 0.5 %project.1.refs_2_.refs_0_ = bf16[128,384]{1,0:T(8,128)(2,1)S(1)} custom-call(s32[1]{0:T(128)} %bitcast.core_ref, bf16[2,64,1536]{2,1,0:T(8,128)(2,1)S(1)} %collective-permute-done.got_ref, s32[2,64]{1,0:T(2,128)S(1)} %collective-permute-done.2.got_ids_ref, bf16[2,64,1536]{2,1,0:T(8,128)(2,1)S(1)} %get-tuple-element.17.own_ref, ...), custom_call_target="tpu_custom_call" | custom-call | flops 150994944 | bytes 1179648 | tf_op jit(solution)/shard_map/project/pallas_call | solution.py:88
  9.4 0.1 collective-permute-start.7
  9.5 0.8 %collective-permute-start.5 = (bf16[128,384]{1,0:T(8,128)(2,1)S(1)}, bf16[128,384]{1,0:T(8,128)(2,1)S(1)}, u32[]{:S(2)}, u32[]{:S(2)}) collective-permute-start(bf16[128,384]{1,0:T(8,128)(2,1)S(1)} %project.1.refs_2_.refs_0_), channel_id=1, source_target_pairs={{0,4},{1,5},{2,6},{3,7},{4,0},{5,1},{6,2},{7,3},{8,12},{9,13},{10,... | collective-permute-start | bytes 294920 | tf_op jit(solution)/shard_map/ppermute | solution.py:25
  10.3 2.4 %fetch.4 = (bf16[1536,1536]{1,0:T(8,128)(2,1)S(1)}, f32[1536]{0:T(1024)S(1)}) custom-call(bf16[1536,1536]{1,0:T(8,128)(2,1)} %refs_0_.4, f32[1536]{0:T(1024)} %refs_1_.4, bf16[128,384]{1,0:T(8,128)(2,1)S(1)} %project.1.refs_2_.refs_0_), custom_call_target="tpu_custom_call" | custom-call | bytes 4721664 | tf_op jit(solution)/shard_map/fetch/pallas_call | solution.py:49
  12.6 2.4 %fetch.5 = (bf16[1536,768]{1,0:T(8,128)(2,1)S(1)}, bf16[768,1536]{1,0:T(8,128)(2,1)S(1)}, bf16[1536]{0:T(1024)(128)(2,1)S(1)}) custom-call(bf16[1536,768]{1,0:T(8,128)(2,1)} %refs_0_.5, bf16[768,1536]{1,0:T(8,128)(2,1)} %refs_1_.5, bf16[1536]{0:T(1024)(128)(2,1)} %refs_2_.3, f32[1536]{0:T(1024)S(1)} %get-tuple-element.22.refs_3_.refs_13_), custom_call_target="tpu_custom_call" | custom-call | bytes 4721664 | tf_op jit(solution)/shard_map/fetch/pallas_call | solution.py:49
  15.0 0.0 collective-permute-done.1.rows_ref
  15.1 0.2 turned.1.mirrored_ref
  15.2 0.1 collective-permute-start.3
  15.3 5.4 %collective-permute-done.7.refs_4_ = bf16[128,384]{1,0:T(8,128)(2,1)S(1)} collective-permute-done((bf16[128,384]{1,0:T(8,128)(2,1)S(1)}, bf16[128,384]{1,0:T(8,128)(2,1)S(1)}, u32[]{:S(2)}, u32[]{:S(2)}) %collective-permute-start.7) | collective-permute-done | bytes 98336 | tf_op jit(solution)/shard_map/ppermute | solution.py:25
  20.7 0.0 collective-permute-start.9
  20.7 0.7 %collective-permute-start.4 = (bf16[128,384]{1,0:T(8,128)(2,1)S(1)}, bf16[128,384]{1,0:T(8,128)(2,1)S(1)}, u32[]{:S(2)}, u32[]{:S(2)}) collective-permute-start(bf16[128,384]{1,0:T(8,128)(2,1)S(1)} %project.1.refs_2_.refs_0_), channel_id=1, source_target_pairs={{0,2},{1,3},{2,0},{3,1},{4,6},{5,7},{6,4},{7,5},{8,10},{9,11},{10,... | collective-permute-start | bytes 294920 | tf_op jit(solution)/shard_map/ppermute | solution.py:25
  21.4 1.3 %collective-permute-start.8 = (bf16[128,384]{1,0:T(8,128)(2,1)S(1)}, bf16[128,384]{1,0:T(8,128)(2,1)S(1)}, u32[]{:S(2)}, u32[]{:S(2)}) collective-permute-start(bf16[128,384]{1,0:T(8,128)(2,1)S(1)} %collective-permute-done.7.refs_4_), channel_id=1, source_target_pairs={{0,2},{1,3},{2,0},{3,1},{4,6},{5,7},{6,4},{7,5},{8,10},{9,11},{10,... | collective-permute-start | bytes 294920 | tf_op jit(solution)/shard_map/ppermute | solution.py:25
  22.7 0.0 collective-permute-done.5.refs_2_
  22.7 0.7 %collective-permute-start.6 = (bf16[128,384]{1,0:T(8,128)(2,1)S(1)}, bf16[128,384]{1,0:T(8,128)(2,1)S(1)}, u32[]{:S(2)}, u32[]{:S(2)}) collective-permute-start(bf16[128,384]{1,0:T(8,128)(2,1)S(1)} %collective-permute-done.5.refs_2_), channel_id=1, source_target_pairs={{0,2},{1,3},{2,0},{3,1},{4,6},{5,7},{6,4},{7,5},{8,10},{9,11},{10,... | collective-permute-start | bytes 294920 | tf_op jit(solution)/shard_map/ppermute | solution.py:25
  23.5 1.9 %collective-permute-done.9.refs_6_ = bf16[128,384]{1,0:T(8,128)(2,1)S(1)} collective-permute-done((bf16[128,384]{1,0:T(8,128)(2,1)S(1)}, bf16[128,384]{1,0:T(8,128)(2,1)S(1)}, u32[]{:S(2)}, u32[]{:S(2)}) %collective-permute-start.9) | collective-permute-done | bytes 98336 | tf_op jit(solution)/shard_map/ppermute | solution.py:25
  25.3 0.5 %collective-permute-start.10 = (bf16[128,384]{1,0:T(8,128)(2,1)S(1)}, bf16[128,384]{1,0:T(8,128)(2,1)S(1)}, u32[]{:S(2)}, u32[]{:S(2)}) collective-permute-start(bf16[128,384]{1,0:T(8,128)(2,1)S(1)} %collective-permute-done.9.refs_6_), channel_id=1, source_target_pairs={{0,2},{1,3},{2,0},{3,1},{4,6},{5,7},{6,4},{7,5},{8,10},{9,11},{10,... | collective-permute-start | bytes 294920 | tf_op jit(solution)/shard_map/ppermute | solution.py:25
  25.9 0.5 %collective-permute-done.4.refs_1_ = bf16[128,384]{1,0:T(8,128)(2,1)S(1)} collective-permute-done((bf16[128,384]{1,0:T(8,128)(2,1)S(1)}, bf16[128,384]{1,0:T(8,128)(2,1)S(1)}, u32[]{:S(2)}, u32[]{:S(2)}) %collective-permute-start.4) | collective-permute-done | bytes 98336 | tf_op jit(solution)/shard_map/ppermute | solution.py:25
  26.4 2.1 %collective-permute-done.8.refs_5_ = bf16[128,384]{1,0:T(8,128)(2,1)S(1)} collective-permute-done((bf16[128,384]{1,0:T(8,128)(2,1)S(1)}, bf16[128,384]{1,0:T(8,128)(2,1)S(1)}, u32[]{:S(2)}, u32[]{:S(2)}) %collective-permute-start.8) | collective-permute-done | bytes 98336 | tf_op jit(solution)/shard_map/ppermute | solution.py:25
  28.5 1.8 %collective-permute-done.6.refs_3_ = bf16[128,384]{1,0:T(8,128)(2,1)S(1)} collective-permute-done((bf16[128,384]{1,0:T(8,128)(2,1)S(1)}, bf16[128,384]{1,0:T(8,128)(2,1)S(1)}, u32[]{:S(2)}, u32[]{:S(2)}) %collective-permute-start.6) | collective-permute-done | bytes 98336 | tf_op jit(solution)/shard_map/ppermute | solution.py:25
  30.3 0.0 collective-permute-done.3.passed_ref
  30.3 1.0 %collective-permute-done.10.refs_7_ = bf16[128,384]{1,0:T(8,128)(2,1)S(1)} collective-permute-done((bf16[128,384]{1,0:T(8,128)(2,1)S(1)}, bf16[128,384]{1,0:T(8,128)(2,1)S(1)}, u32[]{:S(2)}, u32[]{:S(2)}) %collective-permute-start.10) | collective-permute-done | bytes 98336 | tf_op jit(solution)/shard_map/ppermute | solution.py:25
  31.4 0.0 copy-start
  31.4 4.2 %transform.1 = (bf16[64,1536]{1,0:T(8,128)(2,1)S(1)}, bf16[64,1536]{1,0:T(8,128)(2,1)S(1)}) custom-call(s32[1]{0:T(128)} %bitcast.core_ref, bf16[2,64,1536]{2,1,0:T(8,128)(2,1)S(1)} %get-tuple-element.17.own_ref, bf16[2,64,1536]{2,1,0:T(8,128)(2,1)S(1)} %collective-permute-done.got_ref, bf16[64,1536]{1,0:T(8,128)(2,1)S(1)} %turned.1.mirrored_ref, ...), custom_call_target="tpu_custom_call" | custom-call | flops 1610612736 | bytes 9437184 | tf_op jit(solution)/shard_map/transform/pallas_call | solution.py:193
  35.5 0.1 collective-permute-start.11
  35.6 1.4 %collective-permute-done.11.got_ref = bf16[64,1536]{1,0:T(8,128)(2,1)S(1)} collective-permute-done((bf16[64,1536]{1,0:T(8,128)(2,1)S(1)}, bf16[64,1536]{1,0:T(8,128)(2,1)S(1)}, u32[]{:S(2)}, u32[]{:S(2)}) %collective-permute-start.11) | collective-permute-done | bytes 196640 | tf_op jit(solution)/shard_map/ppermute | solution.py:25
  37.1 0.0 copy-done
  37.1 1.5 %combine.1 = f32[64,1536]{1,0:T(8,128)} custom-call(s32[1]{0:T(128)} %bitcast.core_ref, bf16[64,1536]{1,0:T(8,128)(2,1)S(1)} %get-tuple-element.27.keep_ref, bf16[64,1536]{1,0:T(8,128)(2,1)S(1)} %collective-permute-done.11.got_ref, s32[1536]{0:T(1024)S(1)} %copy-done), custom_call_target="tpu_custom_call" | custom-call | tf_op jit(solution)/shard_map/combine/pallas_call | solution.py:236
Async XLA Ops:
  0.0 8.9 %collective-permute-start = (bf16[2,64,1536]{2,1,0:T(8,128)(2,1)}, bf16[2,64,1536]{2,1,0:T(8,128)(2,1)S(1)}, u32[]{:S(2)}, u32[]{:S(2)}) collective-permute-start(bf16[2,64,1536]{2,1,0:T(8,128)(2,1)} %refs_0_.3), channel_id=1, source_target_pairs={{0,1},{1,0},{2,3},{3,2},{4,5},{5,4},{6,7},{7,6},{8,9},{9,8},{10,11... | collective-permute-start | bytes 1179656 | tf_op jit(solution)/shard_map/ppermute | solution.py:25
  2.0 13.1 %collective-permute-start.1 = (bf16[64,1536]{1,0:T(8,128)(2,1)S(1)}, bf16[64,1536]{1,0:T(8,128)(2,1)S(1)}, u32[]{:S(2)}, u32[]{:S(2)}) collective-permute-start(bf16[64,1536]{1,0:T(8,128)(2,1)S(1)} %get-tuple-element.18), channel_id=1, source_target_pairs={{0,14},{1,15},{2,12},{3,13},{4,10},{5,11},{6,8},{7,9},{8,6},{9,7},... | collective-permute-start | bytes 589832 | tf_op jit(solution)/shard_map/ppermute | solution.py:25
  7.6 1.4 %collective-permute-start.2 = (s32[2,64]{1,0:T(2,128)}, s32[2,64]{1,0:T(2,128)S(1)}, u32[]{:S(2)}, u32[]{:S(2)}) collective-permute-start(s32[2,64]{1,0:T(2,128)} %refs_2_.2), channel_id=1, source_target_pairs={{0,1},{1,0},{2,3},{3,2},{4,5},{5,4},{6,7},{7,6},{8,9},{9,8},{10,11... | collective-permute-start | bytes 1544 | tf_op jit(solution)/shard_map/ppermute | solution.py:25
  9.4 11.3 %collective-permute-start.7 = (bf16[128,384]{1,0:T(8,128)(2,1)S(1)}, bf16[128,384]{1,0:T(8,128)(2,1)S(1)}, u32[]{:S(2)}, u32[]{:S(2)}) collective-permute-start(bf16[128,384]{1,0:T(8,128)(2,1)S(1)} %project.1.refs_2_.refs_0_), channel_id=1, source_target_pairs={{0,8},{1,9},{2,10},{3,11},{4,12},{5,13},{6,14},{7,15},{8,0},{9,1},... | collective-permute-start | bytes 294920 | tf_op jit(solution)/shard_map/ppermute | solution.py:25
  9.5 13.2 %collective-permute-start.5 = (bf16[128,384]{1,0:T(8,128)(2,1)S(1)}, bf16[128,384]{1,0:T(8,128)(2,1)S(1)}, u32[]{:S(2)}, u32[]{:S(2)}) collective-permute-start(bf16[128,384]{1,0:T(8,128)(2,1)S(1)} %project.1.refs_2_.refs_0_), channel_id=1, source_target_pairs={{0,4},{1,5},{2,6},{3,7},{4,0},{5,1},{6,2},{7,3},{8,12},{9,13},{10,... | collective-permute-start | bytes 294920 | tf_op jit(solution)/shard_map/ppermute | solution.py:25
  15.2 15.1 %collective-permute-start.3 = (bf16[64,1536]{1,0:T(8,128)(2,1)S(1)}, bf16[64,1536]{1,0:T(8,128)(2,1)S(1)}, u32[]{:S(2)}, u32[]{:S(2)}) collective-permute-start(bf16[64,1536]{1,0:T(8,128)(2,1)S(1)} %turned.1.mirrored_ref), channel_id=1, source_target_pairs={{0,1},{1,0},{2,3},{3,2},{4,5},{5,4},{6,7},{7,6},{8,9},{9,8},{10,11... | collective-permute-start | bytes 589832 | tf_op jit(solution)/shard_map/ppermute | solution.py:25
  20.7 4.6 %collective-permute-start.9 = (bf16[128,384]{1,0:T(8,128)(2,1)S(1)}, bf16[128,384]{1,0:T(8,128)(2,1)S(1)}, u32[]{:S(2)}, u32[]{:S(2)}) collective-permute-start(bf16[128,384]{1,0:T(8,128)(2,1)S(1)} %collective-permute-done.7.refs_4_), channel_id=1, source_target_pairs={{0,4},{1,5},{2,6},{3,7},{4,0},{5,1},{6,2},{7,3},{8,12},{9,13},{10,... | collective-permute-start | bytes 294920 | tf_op jit(solution)/shard_map/ppermute | solution.py:25
  20.7 5.7 %collective-permute-start.4 = (bf16[128,384]{1,0:T(8,128)(2,1)S(1)}, bf16[128,384]{1,0:T(8,128)(2,1)S(1)}, u32[]{:S(2)}, u32[]{:S(2)}) collective-permute-start(bf16[128,384]{1,0:T(8,128)(2,1)S(1)} %project.1.refs_2_.refs_0_), channel_id=1, source_target_pairs={{0,2},{1,3},{2,0},{3,1},{4,6},{5,7},{6,4},{7,5},{8,10},{9,11},{10,... | collective-permute-start | bytes 294920 | tf_op jit(solution)/shard_map/ppermute | solution.py:25
  21.4 7.1 %collective-permute-start.8 = (bf16[128,384]{1,0:T(8,128)(2,1)S(1)}, bf16[128,384]{1,0:T(8,128)(2,1)S(1)}, u32[]{:S(2)}, u32[]{:S(2)}) collective-permute-start(bf16[128,384]{1,0:T(8,128)(2,1)S(1)} %collective-permute-done.7.refs_4_), channel_id=1, source_target_pairs={{0,2},{1,3},{2,0},{3,1},{4,6},{5,7},{6,4},{7,5},{8,10},{9,11},{10,... | collective-permute-start | bytes 294920 | tf_op jit(solution)/shard_map/ppermute | solution.py:25
  22.7 7.6 %collective-permute-start.6 = (bf16[128,384]{1,0:T(8,128)(2,1)S(1)}, bf16[128,384]{1,0:T(8,128)(2,1)S(1)}, u32[]{:S(2)}, u32[]{:S(2)}) collective-permute-start(bf16[128,384]{1,0:T(8,128)(2,1)S(1)} %collective-permute-done.5.refs_2_), channel_id=1, source_target_pairs={{0,2},{1,3},{2,0},{3,1},{4,6},{5,7},{6,4},{7,5},{8,10},{9,11},{10,... | collective-permute-start | bytes 294920 | tf_op jit(solution)/shard_map/ppermute | solution.py:25
  25.3 6.1 %collective-permute-start.10 = (bf16[128,384]{1,0:T(8,128)(2,1)S(1)}, bf16[128,384]{1,0:T(8,128)(2,1)S(1)}, u32[]{:S(2)}, u32[]{:S(2)}) collective-permute-start(bf16[128,384]{1,0:T(8,128)(2,1)S(1)} %collective-permute-done.9.refs_6_), channel_id=1, source_target_pairs={{0,2},{1,3},{2,0},{3,1},{4,6},{5,7},{6,4},{7,5},{8,10},{9,11},{10,... | collective-permute-start | bytes 294920 | tf_op jit(solution)/shard_map/ppermute | solution.py:25
  31.4 5.7 %copy-start = (s32[1536]{0:T(1024)S(1)}, s32[1536]{0:T(1024)}, u32[]{:S(2)}) copy-start(s32[1536]{0:T(1024)} %perm_ref.1) | copy-start | bytes 18436
  35.5 1.5 %collective-permute-start.11 = (bf16[64,1536]{1,0:T(8,128)(2,1)S(1)}, bf16[64,1536]{1,0:T(8,128)(2,1)S(1)}, u32[]{:S(2)}, u32[]{:S(2)}) collective-permute-start(bf16[64,1536]{1,0:T(8,128)(2,1)S(1)} %get-tuple-element.28), channel_id=1, source_target_pairs={{0,1},{1,0},{2,3},{3,2},{4,5},{5,4},{6,7},{7,6},{8,9},{9,8},{10,11... | collective-permute-start | bytes 589832 | tf_op jit(solution)/shard_map/ppermute | solution.py:25

commit v2 on v1

--- a/solution.py
+++ b/solution.py
@@ -154,23 +154,53 @@
     return start
 
 
-def block_kernel(count, core_ref, own_ref, got_ref, mirrored_ref, passed_ref, *refs):
-    kv_refs = refs[:count]
-    gain_ref, wq, wo, head_gain_ref, wh, bias_ref, keep_ref, send_ref = refs[count : count + 8]
-    kv, attended, predictions = refs[count + 8 :]
+def query_kernel(core_ref, own_ref, got_ref, mirrored_ref, passed_ref, gain_ref, weight_ref, query_ref, rows_ref):
     core = core_ref[0]
     half = mirrored_ref.shape[0]
-    head = kv.shape[1] // 2
-    length = pack(kv_refs, kv)
+    head = query_ref.shape[1]
     first = jnp.where(core == 0, own_ref[0].astype(F32), mirrored_ref[...].astype(F32))
     second = jnp.where(core == 0, got_ref[0].astype(F32), passed_ref[...].astype(F32))
     rows = jnp.concatenate([first, second], 0)
+    rows_ref[...] = rows
     normed = normalize(rows, gain_ref[...].astype(F32).reshape(1, -1))
-    queries = jnp.dot(normed, wq[...], preferred_element_type=F32).astype(BF16)
-    for at in range(0, wq.shape[1], head):
-        _, totals, summed = attend(queries[:, at : at + head], kv, length, None)
-        attended[:, at : at + head] = (summed / totals).astype(BF16)
-    summed = rows + jnp.dot(attended[...], wo[...], preferred_element_type=F32)
+    queries = jnp.dot(normed, weight_ref[...], preferred_element_type=F32).astype(BF16)
+    for number in range(weight_ref.shape[1] // head):
+        query_ref[pl.ds(number * 2 * half, 2 * half), :] = queries[:, number * head : (number + 1) * head]
+
+
+def query(core, own, got, mirrored, passed, gain, weight, head):
+    half, width = mirrored.shape
+    heads = weight.shape[1] // head
+    return pl.pallas_call(
+        query_kernel,
+        out_shape=(
+            jax.ShapeDtypeStruct((heads * 2 * half, head), BF16),
+            jax.ShapeDtypeStruct((2 * half, width), F32),
+        ),
+        in_specs=[SMEM] + [VMEM] * 6,
+        out_specs=(VMEM, VMEM),
+        compiler_params=pltpu.CompilerParams(vmem_limit_bytes=10 << 20),
+        cost_estimate=pl.CostEstimate(
+            flops=4 * half * width * weight.shape[1], bytes_accessed=2 * weight.size, transcendentals=0
+        ),
+        name="query",
+    )(core, own, got, mirrored, passed, gain, weight)
+
+
+def block_kernel(count, core_ref, query_ref, rows_ref, *refs):
+    kv_refs = refs[:count]
+    wo, head_gain_ref, wh, bias_ref, keep_ref, send_ref = refs[count : count + 6]
+    kv, attended, predictions = refs[count + 6 :]
+    core = core_ref[0]
+    tokens = rows_ref.shape[0]
+    half = tokens // 2
+    head = query_ref.shape[1]
+    length = pack(kv_refs, kv)
+    _, totals, summed = attend(query_ref[...], kv, length, None)
+    result = (summed / totals).astype(BF16)
+    for number in range(query_ref.shape[0] // tokens):
+        attended[:, number * head : (number + 1) * head] = result[number * tokens : (number + 1) * tokens]
+    summed = rows_ref[...] + jnp.dot(attended[...], wo[...], preferred_element_type=F32)
     normed_out = normalize(summed, head_gain_ref[...].astype(F32).reshape(1, -1))
     tracks = wh.shape[1]
     width = 256
@@ -184,52 +214,54 @@
     send_ref[...] = predictions[pl.ds(pl.multiple_of((1 - core) * half, half), half), :]
 
 
-def transform(core, own, got, mirrored, passed, kvs, gain, wq, wo, head_gain, wh, bias):
-    half, width = mirrored.shape
-    tokens = 2 * half
+def transform(core, queries, rows, kvs, wo, head_gain, wh, bias):
+    tokens, _ = rows.shape
+    head = queries.shape[1]
     length = sum(kv.shape[0] for kv in kvs)
     tracks = wh.shape[1]
-    flops = 2 * tokens * (width * wq.shape[1] * 2 + width * tracks + 2 * length * wq.shape[1])
     return pl.pallas_call(
         functools.partial(block_kernel, len(kvs)),
-        out_shape=(jax.ShapeDtypeStruct((half, tracks), BF16),) * 2,
-        in_specs=[SMEM] + [VMEM] * (10 + len(kvs)),
+        out_shape=(jax.ShapeDtypeStruct((tokens // 2, tracks), BF16),) * 2,
+        in_specs=[SMEM] + [VMEM] * (6 + len(kvs)),
         out_specs=(VMEM, VMEM),
         scratch_shapes=[
-            pltpu.VMEM((length, kvs[0].shape[1]), BF16),
-            pltpu.VMEM((tokens, wq.shape[1]), BF16),
+            pltpu.VMEM((length, 2 * head), BF16),
+            pltpu.VMEM((tokens, wo.shape[0]), BF16),
             pltpu.VMEM((tokens, tracks), BF16),
         ],
         compiler_params=pltpu.CompilerParams(vmem_limit_bytes=28 << 20),
         cost_estimate=pl.CostEstimate(
-            flops=flops,
-            bytes_accessed=2 * (wq.size + wo.size + wh.size),
-            transcendentals=tokens * length * wq.shape[1] * 2 // kvs[0].shape[1],
+            flops=2 * tokens * (wo.size + wh.size) + 4 * queries.size * length,
+            bytes_accessed=2 * (wo.size + wh.size),
+            transcendentals=queries.shape[0] * length,
         ),
         name="transform",
-    )(core, own, got, mirrored, passed, *kvs, gain, wq, wo, head_gain, wh, bias)
-
-
-def combine_kernel(core_ref, keep_ref, got_ref, perm_ref, out_ref):
+    )(core, queries, rows, *kvs, wo, head_gain, wh, bias)
+
+
+def combine_kernel(core_ref, keep_ref, got_ref, perm_ref, out_ref, forward_ref, reverse_ref):
     forward_here = core_ref[0] == 0
+    keep = keep_ref[...].astype(F32)
+    got = got_ref[...].astype(F32)
+    forward_ref[...] = jnp.where(forward_here, keep, got)
+    reverse_ref[...] = jnp.where(forward_here, got, keep)
     tracks = perm_ref.shape[0]
     tokens = keep_ref.shape[0]
     order = perm_ref[...].reshape(1, -1)
     lanes = 128
-    keep = keep_ref[...].astype(F32)
-    got = got_ref[...].astype(F32)
-    forward = jnp.where(forward_here, keep, got)
-    reverse = jnp.where(forward_here, got, keep)
+    group = 8
     for at in range(0, tracks, lanes):
-        perm = jnp.broadcast_to(order[:, at : at + lanes], (tokens, lanes))
+        perm = jnp.broadcast_to(order[:, at : at + lanes], (group, lanes))
         within = perm & (lanes - 1)
         tile = perm >> 7
-        picked = jnp.zeros((tokens, lanes), F32)
-        for number in range(tracks // lanes):
-            source = reverse[:, number * lanes : (number + 1) * lanes]
-            found = jnp.take_along_axis(source, within, axis=1)
-            picked = jnp.where(tile == number, found, picked)
-        out_ref[:, at : at + lanes] = 0.5 * (forward[:, at : at + lanes] + picked)
+        inside = [tile == number for number in range(1, tracks // lanes)]
+        for row in range(0, tokens, group):
+            rows = slice(row, row + group)
+            picked = jnp.take_along_axis(reverse_ref[rows, :lanes], within, axis=1)
+            for number, here in enumerate(inside, 1):
+                source = reverse_ref[rows, number * lanes : (number + 1) * lanes]
+                picked = jnp.where(here, jnp.take_along_axis(source, within, axis=1), picked)
+            out_ref[rows, at : at + lanes] = 0.5 * (forward_ref[rows, at : at + lanes] + picked)
 
 
 def combine(core, keep, got, perm):
@@ -238,6 +270,7 @@
         out_shape=jax.ShapeDtypeStruct(keep.shape, F32),
         in_specs=[SMEM] + [VMEM] * 3,
         out_specs=VMEM,
+        scratch_shapes=[pltpu.VMEM(keep.shape, F32)] * 2,
         compiler_params=pltpu.CompilerParams(vmem_limit_bytes=16 << 20),
         name="combine",
     )(core, keep, got, perm)
@@ -285,12 +318,11 @@
     wq, wo, head_gain = fetch([q_weight, out_weight, head_gain], after=bias)
     mirrored = turned(mirrored, head_gain)
     passed = exchange(mirrored, 1)
-    keep, send = transform(core, own, got, mirrored, passed, kvs, gain, wq, wo, head_gain, wh, bias)
+    queries, rows = query(core, own, got, mirrored, passed, gain, wq, kv.shape[1] // 2)
+    keep, send = transform(core, queries, rows, kvs, wo, head_gain, wh, bias)
     return combine(core, keep, exchange(send, 1), track_perm)
 
 
 def solution(mesh):
     placed = (P("grp", "tok", None), P("grp", "tok"), P(), P(), P(), P(), P(), P(), P(), P())
-    return jax.shard_map(
-        per_device, mesh=mesh, in_specs=placed, out_specs=P(("grp", "tok"), None), check_vma=False
-    )
+    return jax.shard_map(per_device, mesh=mesh, in_specs=placed, out_specs=P(("grp", "tok"), None), check_vma=False)

time: 38.7 us -> 37.8 us (0.977)
  waiting for transfers between devices: 15.4 us -> 8.25 us
  starting transfers between devices: 10.6 us -> 16.9 us
    ppermute x12, waiting for transfers between devices: 15.4 us -> 8.25 us  [exchange(): return lax.ppermute(value, 'tok', [(s, s ^ mask) for s in range(count)])]
    ppermute x12, starting transfers between devices: 10.6 us -> 16.9 us  [exchange(): return lax.ppermute(value, 'tok', [(s, s ^ mask) for s in range(count)])]
    pallas_call x1, Pallas kernels: 4.16 us -> 3.32 us  [transform(): pl.pallas_call(functools.partial(block_kernel, len(kvs)), out_shape=(jax....]
    pallas_call x0 -> x1, Pallas kernels: none -> 0.75 us  [query(): pl.pallas_call(query_kernel, out_shape=(jax.ShapeDtypeStruct((heads * 2 *...]
  transfers between devices with their start and end apart: 12 -> 12, of which waited for: 8 -> 8; matrix products, arithmetic and copies ran while one was open for 0% -> 0% of each run, Pallas kernels for 18% -> 20%
where the time goes in v2:
time: 37.8 us; the launch traced here: 37.7 us
  starting transfers between devices  16.9 us (45%)
  Pallas kernels  12.4 us (33%)
  waiting for transfers between devices  8.25 us (22%)
    ppermute x12, starting transfers between devices, exchange(): return lax.ppermute(value, 'tok', [(s, s ^ mask) for s in range(count)])  16.9 us
    ppermute x12, waiting for transfers between devices, exchange(): return lax.ppermute(value, 'tok', [(s, s ^ mask) for s in range(count)])  8.25 us
    pallas_call x3, Pallas kernels, fetch(): pl.pallas_call(functools.partial(fetch_kernel, places), out_shape=[jax.Sh...  6.24 us
    pallas_call x1, Pallas kernels, transform(): pl.pallas_call(functools.partial(block_kernel, len(kvs)), out_shape=(jax....  3.32 us
    pallas_call x1, Pallas kernels, combine(): pl.pallas_call(combine_kernel, out_shape=jax.ShapeDtypeStruct(keep.shape,...  1.46 us
  transfers between devices with their start and end apart: 12, of which 8 were waited for; matrix products, arithmetic and copies ran while one was open for 0% of the time, Pallas kernels for 20%

profile of v2, /device:TPU:0, one launch (start us, length us, event | category | flops | bytes accessed | tf_op | source)
XLA Modules:
  0.0 37.7 jit_solution(17842853009452380952)
XLA Ops:
  0.0 0.5 %collective-permute-start = (bf16[2,64,1536]{2,1,0:T(8,128)(2,1)}, bf16[2,64,1536]{2,1,0:T(8,128)(2,1)S(1)}, u32[]{:S(2)}, u32[]{:S(2)}) collective-permute-start(bf16[2,64,1536]{2,1,0:T(8,128)(2,1)} %refs_0_.3), channel_id=1, source_target_pairs={{0,1},{1,0},{2,3},{3,2},{4,5},{5,4},{6,7},{7,6},{8,9},{9,8},{10,11... | collective-permute-start | bytes 1179656 | tf_op jit(solution)/shard_map/ppermute | solution.py:25
  0.5 1.5 %fetch.3 = (bf16[2,64,1536]{2,1,0:T(8,128)(2,1)S(1)}, bf16[1536]{0:T(1024)(128)(2,1)S(1)}, s32[2,64]{1,0:T(2,128)S(1)}, bf16[1536,384]{1,0:T(8,128)(2,1)S(1)}, bf16[64,1536]{1,0:T(8,128)(2,1)S(1)}) custom-call(bf16[2,64,1536]{2,1,0:T(8,128)(2,1)} %refs_0_.3, bf16[1536]{0:T(1024)(128)(2,1)} %refs_1_.3, s32[2,64]{1,0:T(2,128)} %refs_2_.2, ...), custom_call_target="tpu_custom_call" | custom-call | bytes 1576192 | tf_op jit(solution)/shard_map/fetch/pallas_call | solution.py:49
  2.0 5.6 %collective-permute-start.1 = (bf16[64,1536]{1,0:T(8,128)(2,1)S(1)}, bf16[64,1536]{1,0:T(8,128)(2,1)S(1)}, u32[]{:S(2)}, u32[]{:S(2)}) collective-permute-start(bf16[64,1536]{1,0:T(8,128)(2,1)S(1)} %get-tuple-element.20), channel_id=1, source_target_pairs={{0,14},{1,15},{2,12},{3,13},{4,10},{5,11},{6,8},{7,9},{8,6},{9,7},... | collective-permute-start | bytes 589832 | tf_op jit(solution)/shard_map/ppermute | solution.py:25
  7.6 0.2 collective-permute-start.2
  7.8 1.1 %collective-permute-done.2.got_ids_ref = s32[2,64]{1,0:T(2,128)S(1)} collective-permute-done((s32[2,64]{1,0:T(2,128)}, s32[2,64]{1,0:T(2,128)S(1)}, u32[]{:S(2)}, u32[]{:S(2)}) %collective-permute-start.2) | collective-permute-done | bytes 544 | tf_op jit(solution)/shard_map/ppermute | solution.py:25
  8.9 0.0 collective-permute-done.got_ref
  8.9 0.5 %project.1.refs_2_.refs_0_ = bf16[128,384]{1,0:T(8,128)(2,1)S(1)} custom-call(s32[1]{0:T(128)} %bitcast.core_ref, bf16[2,64,1536]{2,1,0:T(8,128)(2,1)S(1)} %collective-permute-done.got_ref, s32[2,64]{1,0:T(2,128)S(1)} %collective-permute-done.2.got_ids_ref, bf16[2,64,1536]{2,1,0:T(8,128)(2,1)S(1)} %get-tuple-element.19.own_ref, ...), custom_call_target="tpu_custom_call" | custom-call | flops 150994944 | bytes 1179648 | tf_op jit(solution)/shard_map/project/pallas_call | solution.py:88
  9.4 0.1 collective-permute-start.7
  9.5 2.4 %fetch.4 = (bf16[1536,1536]{1,0:T(8,128)(2,1)S(1)}, f32[1536]{0:T(1024)S(1)}) custom-call(bf16[1536,1536]{1,0:T(8,128)(2,1)} %refs_0_.4, f32[1536]{0:T(1024)} %refs_1_.4, bf16[128,384]{1,0:T(8,128)(2,1)S(1)} %project.1.refs_2_.refs_0_), custom_call_target="tpu_custom_call" | custom-call | bytes 4721664 | tf_op jit(solution)/shard_map/fetch/pallas_call | solution.py:49
  11.9 2.4 %fetch.5 = (bf16[1536,768]{1,0:T(8,128)(2,1)S(1)}, bf16[768,1536]{1,0:T(8,128)(2,1)S(1)}, bf16[1536]{0:T(1024)(128)(2,1)S(1)}) custom-call(bf16[1536,768]{1,0:T(8,128)(2,1)} %refs_0_.5, bf16[768,1536]{1,0:T(8,128)(2,1)} %refs_1_.5, bf16[1536]{0:T(1024)(128)(2,1)} %refs_2_.3, f32[1536]{0:T(1024)S(1)} %get-tuple-element.24.refs_3_.refs_11_), custom_call_target="tpu_custom_call" | custom-call | bytes 4721664 | tf_op jit(solution)/shard_map/fetch/pallas_call | solution.py:49
  14.3 0.0 collective-permute-done.1.rows_ref
  14.3 0.2 turned.1.mirrored_ref
  14.5 0.3 collective-permute-start.3
  14.8 5.2 %collective-permute-start.5 = (bf16[128,384]{1,0:T(8,128)(2,1)S(1)}, bf16[128,384]{1,0:T(8,128)(2,1)S(1)}, u32[]{:S(2)}, u32[]{:S(2)}) collective-permute-start(bf16[128,384]{1,0:T(8,128)(2,1)S(1)} %project.1.refs_2_.refs_0_), channel_id=1, source_target_pairs={{0,4},{1,5},{2,6},{3,7},{4,0},{5,1},{6,2},{7,3},{8,12},{9,13},{10,... | collective-permute-start | bytes 294920 | tf_op jit(solution)/shard_map/ppermute | solution.py:25
  19.9 0.8 %collective-permute-done.7.refs_4_ = bf16[128,384]{1,0:T(8,128)(2,1)S(1)} collective-permute-done((bf16[128,384]{1,0:T(8,128)(2,1)S(1)}, bf16[128,384]{1,0:T(8,128)(2,1)S(1)}, u32[]{:S(2)}, u32[]{:S(2)}) %collective-permute-start.7) | collective-permute-done | bytes 98336 | tf_op jit(solution)/shard_map/ppermute | solution.py:25
  20.7 0.0 collective-permute-start.9
  20.7 0.8 %collective-permute-start.4 = (bf16[128,384]{1,0:T(8,128)(2,1)S(1)}, bf16[128,384]{1,0:T(8,128)(2,1)S(1)}, u32[]{:S(2)}, u32[]{:S(2)}) collective-permute-start(bf16[128,384]{1,0:T(8,128)(2,1)S(1)} %project.1.refs_2_.refs_0_), channel_id=1, source_target_pairs={{0,2},{1,3},{2,0},{3,1},{4,6},{5,7},{6,4},{7,5},{8,10},{9,11},{10,... | collective-permute-start | bytes 294920 | tf_op jit(solution)/shard_map/ppermute | solution.py:25
  21.5 1.2 %collective-permute-start.8 = (bf16[128,384]{1,0:T(8,128)(2,1)S(1)}, bf16[128,384]{1,0:T(8,128)(2,1)S(1)}, u32[]{:S(2)}, u32[]{:S(2)}) collective-permute-start(bf16[128,384]{1,0:T(8,128)(2,1)S(1)} %collective-permute-done.7.refs_4_), channel_id=1, source_target_pairs={{0,2},{1,3},{2,0},{3,1},{4,6},{5,7},{6,4},{7,5},{8,10},{9,11},{10,... | collective-permute-start | bytes 294920 | tf_op jit(solution)/shard_map/ppermute | solution.py:25
  22.7 0.8 %collective-permute-done.5.refs_2_ = bf16[128,384]{1,0:T(8,128)(2,1)S(1)} collective-permute-done((bf16[128,384]{1,0:T(8,128)(2,1)S(1)}, bf16[128,384]{1,0:T(8,128)(2,1)S(1)}, u32[]{:S(2)}, u32[]{:S(2)}) %collective-permute-start.5) | collective-permute-done | bytes 98336 | tf_op jit(solution)/shard_map/ppermute | solution.py:25
  23.6 1.5 %collective-permute-start.6 = (bf16[128,384]{1,0:T(8,128)(2,1)S(1)}, bf16[128,384]{1,0:T(8,128)(2,1)S(1)}, u32[]{:S(2)}, u32[]{:S(2)}) collective-permute-start(bf16[128,384]{1,0:T(8,128)(2,1)S(1)} %collective-permute-done.5.refs_2_), channel_id=1, source_target_pairs={{0,2},{1,3},{2,0},{3,1},{4,6},{5,7},{6,4},{7,5},{8,10},{9,11},{10,... | collective-permute-start | bytes 294920 | tf_op jit(solution)/shard_map/ppermute | solution.py:25
  25.1 0.4 collective-permute-done.9.refs_6_
  25.4 1.5 %collective-permute-start.10 = (bf16[128,384]{1,0:T(8,128)(2,1)S(1)}, bf16[128,384]{1,0:T(8,128)(2,1)S(1)}, u32[]{:S(2)}, u32[]{:S(2)}) collective-permute-start(bf16[128,384]{1,0:T(8,128)(2,1)S(1)} %collective-permute-done.9.refs_6_), channel_id=1, source_target_pairs={{0,2},{1,3},{2,0},{3,1},{4,6},{5,7},{6,4},{7,5},{8,10},{9,11},{10,... | collective-permute-start | bytes 294920 | tf_op jit(solution)/shard_map/ppermute | solution.py:25
  26.9 0.0 collective-permute-done.3.passed_ref
  26.9 0.7 %query.1 = (bf16[512,192]{1,0:T(8,128)(2,1)S(1)}, f32[128,1536]{1,0:T(8,128)S(1)}) custom-call(s32[1]{0:T(128)} %bitcast.core_ref, bf16[2,64,1536]{2,1,0:T(8,128)(2,1)S(1)} %get-tuple-element.19.own_ref, bf16[2,64,1536]{2,1,0:T(8,128)(2,1)S(1)} %collective-permute-done.got_ref, bf16[64,1536]{1,0:T(8,128)(2,1)S(1)} %turned.1.mirrored_ref, ...), custom_call_target="tpu_custom_call" | custom-call | flops 301989888 | bytes 2359296 | tf_op jit(solution)/shard_map/query/pallas_call | solution.py:174
  27.7 0.0 collective-permute-done.4.refs_1_
  27.7 0.8 %collective-permute-done.8.refs_5_ = bf16[128,384]{1,0:T(8,128)(2,1)S(1)} collective-permute-done((bf16[128,384]{1,0:T(8,128)(2,1)S(1)}, bf16[128,384]{1,0:T(8,128)(2,1)S(1)}, u32[]{:S(2)}, u32[]{:S(2)}) %collective-permute-start.8) | collective-permute-done | bytes 98336 | tf_op jit(solution)/shard_map/ppermute | solution.py:25
  28.5 1.8 %collective-permute-done.6.refs_3_ = bf16[128,384]{1,0:T(8,128)(2,1)S(1)} collective-permute-done((bf16[128,384]{1,0:T(8,128)(2,1)S(1)}, bf16[128,384]{1,0:T(8,128)(2,1)S(1)}, u32[]{:S(2)}, u32[]{:S(2)}) %collective-permute-start.6) | collective-permute-done | bytes 98336 | tf_op jit(solution)/shard_map/ppermute | solution.py:25
  30.3 1.1 %collective-permute-done.10.refs_7_ = bf16[128,384]{1,0:T(8,128)(2,1)S(1)} collective-permute-done((bf16[128,384]{1,0:T(8,128)(2,1)S(1)}, bf16[128,384]{1,0:T(8,128)(2,1)S(1)}, u32[]{:S(2)}, u32[]{:S(2)}) %collective-permute-start.10) | collective-permute-done | bytes 98336 | tf_op jit(solution)/shard_map/ppermute | solution.py:25
  31.4 0.0 copy-start
  31.4 3.3 %transform.1 = (bf16[64,1536]{1,0:T(8,128)(2,1)S(1)}, bf16[64,1536]{1,0:T(8,128)(2,1)S(1)}) custom-call(s32[1]{0:T(128)} %bitcast.core_ref, bf16[512,192]{1,0:T(8,128)(2,1)S(1)} %get-tuple-element.27.query_ref, f32[128,1536]{1,0:T(8,128)S(1)} %get-tuple-element.28.rows_ref, bf16[128,384]{1,0:T(8,128)(2,1)S(1)} %project.1.refs_2_.refs_0_, ...), custom_call_target="tpu_custom_call" | custom-call | flops 1308622848 | bytes 7077888 | tf_op jit(solution)/shard_map/transform/pallas_call | solution.py:222
  34.7 0.1 collective-permute-start.11
  34.8 1.4 %collective-permute-done.11.got_ref = bf16[64,1536]{1,0:T(8,128)(2,1)S(1)} collective-permute-done((bf16[64,1536]{1,0:T(8,128)(2,1)S(1)}, bf16[64,1536]{1,0:T(8,128)(2,1)S(1)}, u32[]{:S(2)}, u32[]{:S(2)}) %collective-permute-start.11) | collective-permute-done | bytes 196640 | tf_op jit(solution)/shard_map/ppermute | solution.py:25
  36.2 0.0 copy-done
  36.2 1.5 %combine.1 = f32[64,1536]{1,0:T(8,128)} custom-call(s32[1]{0:T(128)} %bitcast.core_ref, bf16[64,1536]{1,0:T(8,128)(2,1)S(1)} %get-tuple-element.31.keep_ref, bf16[64,1536]{1,0:T(8,128)(2,1)S(1)} %collective-permute-done.11.got_ref, s32[1536]{0:T(1024)S(1)} %copy-done), custom_call_target="tpu_custom_call" | custom-call | tf_op jit(solution)/shard_map/combine/pallas_call | solution.py:268
Async XLA Ops:
  0.0 8.9 %collective-permute-start = (bf16[2,64,1536]{2,1,0:T(8,128)(2,1)}, bf16[2,64,1536]{2,1,0:T(8,128)(2,1)S(1)}, u32[]{:S(2)}, u32[]{:S(2)}) collective-permute-start(bf16[2,64,1536]{2,1,0:T(8,128)(2,1)} %refs_0_.3), channel_id=1, source_target_pairs={{0,1},{1,0},{2,3},{3,2},{4,5},{5,4},{6,7},{7,6},{8,9},{9,8},{10,11... | collective-permute-start | bytes 1179656 | tf_op jit(solution)/shard_map/ppermute | solution.py:25
  2.0 12.3 %collective-permute-start.1 = (bf16[64,1536]{1,0:T(8,128)(2,1)S(1)}, bf16[64,1536]{1,0:T(8,128)(2,1)S(1)}, u32[]{:S(2)}, u32[]{:S(2)}) collective-permute-start(bf16[64,1536]{1,0:T(8,128)(2,1)S(1)} %get-tuple-element.20), channel_id=1, source_target_pairs={{0,14},{1,15},{2,12},{3,13},{4,10},{5,11},{6,8},{7,9},{8,6},{9,7},... | collective-permute-start | bytes 589832 | tf_op jit(solution)/shard_map/ppermute | solution.py:25
  7.6 1.4 %collective-permute-start.2 = (s32[2,64]{1,0:T(2,128)}, s32[2,64]{1,0:T(2,128)S(1)}, u32[]{:S(2)}, u32[]{:S(2)}) collective-permute-start(s32[2,64]{1,0:T(2,128)} %refs_2_.2), channel_id=1, source_target_pairs={{0,1},{1,0},{2,3},{3,2},{4,5},{5,4},{6,7},{7,6},{8,9},{9,8},{10,11... | collective-permute-start | bytes 1544 | tf_op jit(solution)/shard_map/ppermute | solution.py:25
  9.4 11.3 %collective-permute-start.7 = (bf16[128,384]{1,0:T(8,128)(2,1)S(1)}, bf16[128,384]{1,0:T(8,128)(2,1)S(1)}, u32[]{:S(2)}, u32[]{:S(2)}) collective-permute-start(bf16[128,384]{1,0:T(8,128)(2,1)S(1)} %project.1.refs_2_.refs_0_), channel_id=1, source_target_pairs={{0,8},{1,9},{2,10},{3,11},{4,12},{5,13},{6,14},{7,15},{8,0},{9,1},... | collective-permute-start | bytes 294920 | tf_op jit(solution)/shard_map/ppermute | solution.py:25
  14.5 12.4 %collective-permute-start.3 = (bf16[64,1536]{1,0:T(8,128)(2,1)S(1)}, bf16[64,1536]{1,0:T(8,128)(2,1)S(1)}, u32[]{:S(2)}, u32[]{:S(2)}) collective-permute-start(bf16[64,1536]{1,0:T(8,128)(2,1)S(1)} %turned.1.mirrored_ref), channel_id=1, source_target_pairs={{0,1},{1,0},{2,3},{3,2},{4,5},{5,4},{6,7},{7,6},{8,9},{9,8},{10,11... | collective-permute-start | bytes 589832 | tf_op jit(solution)/shard_map/ppermute | solution.py:25
  14.8 8.8 %collective-permute-start.5 = (bf16[128,384]{1,0:T(8,128)(2,1)S(1)}, bf16[128,384]{1,0:T(8,128)(2,1)S(1)}, u32[]{:S(2)}, u32[]{:S(2)}) collective-permute-start(bf16[128,384]{1,0:T(8,128)(2,1)S(1)} %project.1.refs_2_.refs_0_), channel_id=1, source_target_pairs={{0,4},{1,5},{2,6},{3,7},{4,0},{5,1},{6,2},{7,3},{8,12},{9,13},{10,... | collective-permute-start | bytes 294920 | tf_op jit(solution)/shard_map/ppermute | solution.py:25
  20.7 4.7 %collective-permute-start.9 = (bf16[128,384]{1,0:T(8,128)(2,1)S(1)}, bf16[128,384]{1,0:T(8,128)(2,1)S(1)}, u32[]{:S(2)}, u32[]{:S(2)}) collective-permute-start(bf16[128,384]{1,0:T(8,128)(2,1)S(1)} %collective-permute-done.7.refs_4_), channel_id=1, source_target_pairs={{0,4},{1,5},{2,6},{3,7},{4,0},{5,1},{6,2},{7,3},{8,12},{9,13},{10,... | collective-permute-start | bytes 294920 | tf_op jit(solution)/shard_map/ppermute | solution.py:25
  20.7 7.0 %collective-permute-start.4 = (bf16[128,384]{1,0:T(8,128)(2,1)S(1)}, bf16[128,384]{1,0:T(8,128)(2,1)S(1)}, u32[]{:S(2)}, u32[]{:S(2)}) collective-permute-start(bf16[128,384]{1,0:T(8,128)(2,1)S(1)} %project.1.refs_2_.refs_0_), channel_id=1, source_target_pairs={{0,2},{1,3},{2,0},{3,1},{4,6},{5,7},{6,4},{7,5},{8,10},{9,11},{10,... | collective-permute-start | bytes 294920 | tf_op jit(solution)/shard_map/ppermute | solution.py:25
  21.5 7.0 %collective-permute-start.8 = (bf16[128,384]{1,0:T(8,128)(2,1)S(1)}, bf16[128,384]{1,0:T(8,128)(2,1)S(1)}, u32[]{:S(2)}, u32[]{:S(2)}) collective-permute-start(bf16[128,384]{1,0:T(8,128)(2,1)S(1)} %collective-permute-done.7.refs_4_), channel_id=1, source_target_pairs={{0,2},{1,3},{2,0},{3,1},{4,6},{5,7},{6,4},{7,5},{8,10},{9,11},{10,... | collective-permute-start | bytes 294920 | tf_op jit(solution)/shard_map/ppermute | solution.py:25
  23.6 6.8 %collective-permute-start.6 = (bf16[128,384]{1,0:T(8,128)(2,1)S(1)}, bf16[128,384]{1,0:T(8,128)(2,1)S(1)}, u32[]{:S(2)}, u32[]{:S(2)}) collective-permute-start(bf16[128,384]{1,0:T(8,128)(2,1)S(1)} %collective-permute-done.5.refs_2_), channel_id=1, source_target_pairs={{0,2},{1,3},{2,0},{3,1},{4,6},{5,7},{6,4},{7,5},{8,10},{9,11},{10,... | collective-permute-start | bytes 294920 | tf_op jit(solution)/shard_map/ppermute | solution.py:25
  25.4 6.0 %collective-permute-start.10 = (bf16[128,384]{1,0:T(8,128)(2,1)S(1)}, bf16[128,384]{1,0:T(8,128)(2,1)S(1)}, u32[]{:S(2)}, u32[]{:S(2)}) collective-permute-start(bf16[128,384]{1,0:T(8,128)(2,1)S(1)} %collective-permute-done.9.refs_6_), channel_id=1, source_target_pairs={{0,2},{1,3},{2,0},{3,1},{4,6},{5,7},{6,4},{7,5},{8,10},{9,11},{10,... | collective-permute-start | bytes 294920 | tf_op jit(solution)/shard_map/ppermute | solution.py:25
  31.4 4.8 %copy-start = (s32[1536]{0:T(1024)S(1)}, s32[1536]{0:T(1024)}, u32[]{:S(2)}) copy-start(s32[1536]{0:T(1024)} %perm_ref.1) | copy-start | bytes 18436
  34.7 1.5 %collective-permute-start.11 = (bf16[64,1536]{1,0:T(8,128)(2,1)S(1)}, bf16[64,1536]{1,0:T(8,128)(2,1)S(1)}, u32[]{:S(2)}, u32[]{:S(2)}) collective-permute-start(bf16[64,1536]{1,0:T(8,128)(2,1)S(1)} %get-tuple-element.32), channel_id=1, source_target_pairs={{0,1},{1,0},{2,3},{3,2},{4,5},{5,4},{6,7},{7,6},{8,9},{9,8},{10,11... | collective-permute-start | bytes 589832 | tf_op jit(solution)/shard_map/ppermute | solution.py:25

commit v3 on v2

v3 whole, which is shorter than its diff:
```python
import functools
import math

import jax
import jax.numpy as jnp
from jax import lax
from jax.experimental import pallas as pl
from jax.experimental.pallas import tpu as pltpu
from jax.sharding import PartitionSpec as P

VMEM = pl.BlockSpec(memory_space=pltpu.VMEM)
SMEM = pl.BlockSpec(memory_space=pltpu.SMEM)
HBM = pl.BlockSpec(memory_space=pltpu.HBM)
ANY = pl.BlockSpec(memory_space=pl.ANY)
F32 = jnp.float32
BF16 = jnp.bfloat16


def in_hbm(value):
    return pltpu.with_memory_space_constraint(value, pltpu.HBM)


def exchange(value, mask):
    count = lax.axis_size("tok")
    return lax.ppermute(value, "tok", [(s, s ^ mask) for s in range(count)])


def normalize(rows, gain):
    mean = jnp.mean(rows * rows, -1, keepdims=True)
    return (rows * lax.rsqrt(mean + 1e-06) * gain).astype(BF16)


def fetch_kernel(count, *refs):
    *refs, sems = refs
    copies = [
        pltpu.make_async_copy(source, target, sems.at[number])
        for number, (source, target) in enumerate(zip(refs[:count], refs[-count:]))
    ]
    for copy in copies:
        copy.start()
    for copy in copies:
        copy.wait()


def fetch(values, after=None):
    waited = [] if after is None else [after]
    return pl.pallas_call(
        functools.partial(fetch_kernel, len(values)),
        out_shape=[jax.ShapeDtypeStruct(value.shape, value.dtype) for value in values],
        in_specs=[HBM] * len(values) + [ANY] * len(waited),
        out_specs=[VMEM] * len(values),
        scratch_shapes=[pltpu.SemaphoreType.DMA((len(values),))],
        compiler_params=pltpu.CompilerParams(vmem_limit_bytes=1 << 20),
        cost_estimate=pl.CostEstimate(
            flops=0, bytes_accessed=sum(2 * value.size for value in values), transcendentals=0
        ),
        name="fetch",
    )(*[in_hbm(value) for value in values], *waited)


def project_kernel(core_ref, got_ref, got_ids_ref, own_ref, own_ids_ref, gain_ref, weight_ref, kv_ref, turned_ref):
    core = core_ref[0]
    tokens = own_ref.shape[1]
    head = weight_ref.shape[1] // 2
    gain = gain_ref[...].astype(F32).reshape(1, -1)
    row = lax.broadcasted_iota(jnp.int32, (tokens, tokens), 0)
    col = lax.broadcasted_iota(jnp.int32, (tokens, tokens), 1)
    lane = lax.broadcasted_iota(jnp.int32, (tokens, weight_ref.shape[1]), 1)
    normed, left_out = [], []
    for ref, ids_ref in ((own_ref, own_ids_ref), (got_ref, got_ids_ref)):
        ids = jnp.where(core == 0, ids_ref[0:1, :], ids_ref[1:2, :])
        unknown = jnp.where((row == col) & (ids == 4), 1.0, 0.0)
        left_out.append((lane < head) & (jnp.max(unknown, -1, keepdims=True) > 0.5))
        normed.append(normalize(ref[core].astype(F32), gain))
    turn = jnp.where(row + col == tokens - 1, 1.0, 0.0).astype(BF16)
    turned_ref[...] = jnp.dot(turn, own_ref[1], preferred_element_type=F32).astype(BF16)
    kv = jnp.dot(jnp.concatenate(normed, 0), weight_ref[...], preferred_element_type=F32)
    for part in range(2):
        kv_ref[pl.ds(part * tokens, tokens), :] = jnp.where(
            left_out[part], jnp.nan, kv[part * tokens : (part + 1) * tokens]
        ).astype(BF16)


def project(core, got, got_ids, own, own_ids, gain, weight):
    tokens, width = own.shape[1:]
    return pl.pallas_call(
        project_kernel,
        out_shape=(
            jax.ShapeDtypeStruct((2 * tokens, weight.shape[1]), BF16),
            jax.ShapeDtypeStruct((tokens, width), BF16),
        ),
        in_specs=[SMEM] + [VMEM] * 6,
        out_specs=(VMEM, VMEM),
        compiler_params=pltpu.CompilerParams(vmem_limit_bytes=12 << 20),
        cost_estimate=pl.CostEstimate(
            flops=4 * tokens * width * weight.shape[1], bytes_accessed=2 * weight.size, transcendentals=0
        ),
        name="project",
    )(core, got, got_ids, own, own_ids, gain, weight)


def attend(queries, segments, head):
    rate = math.log2(math.e) / math.sqrt(head)
    chunk = 1024

    def step(parts, state):
        scores = [
            lax.dot_general(queries, keys, (((1,), (1,)), ((), ())), preferred_element_type=F32)
            for keys, _ in parts
        ]
        maxima = functools.reduce(jnp.maximum, [jnp.max(part, -1, keepdims=True) for part in scores])
        if state is not None:
            maxima = jnp.maximum(maxima, state[0])
        weights = [jnp.exp2((part - maxima) * rate) for part in scores]
        totals = sum(jnp.sum(part, -1, keepdims=True) for part in weights)
        summed = sum(
            jnp.dot(part.astype(BF16), values, preferred_element_type=F32)
            for part, (_, values) in zip(weights, parts)
        )
        if state is not None:
            kept = jnp.exp2((state[0] - maxima) * rate)
            totals = totals + state[1] * kept
            summed = summed + state[2] * kept
        return maxima, totals, summed

    if sum(keys.shape[0] for keys, _ in segments) <= chunk:
        return step([(keys[...], values[...]) for keys, values in segments], None)
    keys, values = segments[0]

    def one(position, state):
        at = pl.ds(pl.multiple_of(position * chunk, chunk), chunk)
        return step([(keys[at, :], values[at, :])], state)

    return lax.fori_loop(1, keys.shape[0] // chunk, one, one(0, None))


def pack(kv_refs, keys, values):
    head = values.shape[1]
    start = 0
    for ref in kv_refs:
        rows = ref.shape[0]
        at = pl.ds(start, rows)
        key = ref[:, :head].astype(F32)
        known = key == key
        keys[at, :head] = jnp.where(known, key, 0.0).astype(BF16)
        keys[at, head:] = jnp.where(known[:, : keys.shape[1] - head], 0.0, -1e30).astype(BF16)
        values[at, :] = ref[:, head:]
        start += rows
    return start


def padded(head):
    return head // 128 * 128 + 128


def pack_kernel(*refs):
    *kv_refs, keys_ref, values_ref = refs
    pack(kv_refs, keys_ref, values_ref)


def packed(kvs):
    head = kvs[0].shape[1] // 2
    length = sum(kv.shape[0] for kv in kvs)
    return pl.pallas_call(
        pack_kernel,
        out_shape=(
            jax.ShapeDtypeStruct((length, padded(head)), BF16),
            jax.ShapeDtypeStruct((length, head), BF16),
        ),
        in_specs=[VMEM] * len(kvs),
        out_specs=(VMEM, VMEM),
        compiler_params=pltpu.CompilerParams(vmem_limit_bytes=2 << 20),
        name="packed",
    )(*kvs)


def query_kernel(head, core_ref, own_ref, got_ref, mirrored_ref, passed_ref, gain_ref, weight_ref, query_ref, rows_ref):
    core = core_ref[0]
    half = mirrored_ref.shape[0]
    first = jnp.where(core == 0, own_ref[0].astype(F32), mirrored_ref[...].astype(F32))
    second = jnp.where(core == 0, got_ref[0].astype(F32), passed_ref[...].astype(F32))
    rows = jnp.concatenate([first, second], 0)
    rows_ref[...] = rows
    normed = normalize(rows, gain_ref[...].astype(F32).reshape(1, -1))
    queries = jnp.dot(normed, weight_ref[...], preferred_element_type=F32).astype(BF16)
    lane = lax.broadcasted_iota(jnp.int32, (2 * half, query_ref.shape[1] - head), 1)
    for number in range(weight_ref.shape[1] // head):
        at = pl.ds(number * 2 * half, 2 * half)
        query_ref[at, :head] = queries[:, number * head : (number + 1) * head]
        query_ref[at, head:] = jnp.where(lane == 0, 1.0, 0.0).astype(BF16)


def query(core, own, got, mirrored, passed, gain, weight, head):
    half, width = mirrored.shape
    heads = weight.shape[1] // head
    return pl.pallas_call(
        functools.partial(query_kernel, head),
        out_shape=(
            jax.ShapeDtypeStruct((heads * 2 * half, padded(head)), BF16),
            jax.ShapeDtypeStruct((2 * half, width), F32),
        ),
        in_specs=[SMEM] + [VMEM] * 6,
        out_specs=(VMEM, VMEM),
        compiler_params=pltpu.CompilerParams(vmem_limit_bytes=10 << 20),
        cost_estimate=pl.CostEstimate(
            flops=4 * half * width * weight.shape[1], bytes_accessed=2 * weight.size, transcendentals=0
        ),
        name="query",
    )(core, own, got, mirrored, passed, gain, weight)


def block_kernel(count, core_ref, query_ref, rows_ref, *refs):
    kv_refs = refs[:count]
    early = refs[count : len(refs) - 10]
    wo, head_gain_ref, wh, bias_ref, keep_ref, send_ref, keys, values, attended, predictions = refs[-10:]
    core = core_ref[0]
    tokens = rows_ref.shape[0]
    half = tokens // 2
    head = values.shape[1]
    pack(kv_refs, keys, values)
    segments = ([early] if early else []) + [(keys, values)]
    heads = query_ref.shape[0] // tokens
    group = 2 if heads % 2 == 0 else 1
    for first in range(0, heads, group):
        _, totals, summed = attend(
            query_ref[pl.ds(first * tokens, group * tokens), :], segments, head
        )
        result = (summed / totals).astype(BF16)
        for number in range(group):
            at = (first + number) * head
            attended[:, at : at + head] = result[number * tokens : (number + 1) * tokens]
    summed = rows_ref[...] + jnp.dot(attended[...], wo[...], preferred_element_type=F32)
    normed_out = normalize(summed, head_gain_ref[...].astype(F32).reshape(1, -1))
    tracks = wh.shape[1]
    width = 256
    bias = bias_ref[...].reshape(1, -1)
    for at in range(0, tracks, width):
        logits = jnp.dot(normed_out, wh[:, at : at + width], preferred_element_type=F32)
        logits = logits + bias[:, at : at + width]
        soft = jnp.maximum(logits, 0.0) + jnp.log1p(jnp.exp(-jnp.abs(logits)))
        predictions[:, at : at + width] = soft.astype(BF16)
    keep_ref[...] = predictions[pl.ds(pl.multiple_of(core * half, half), half), :]
    send_ref[...] = predictions[pl.ds(pl.multiple_of((1 - core) * half, half), half), :]


def transform(core, queries, rows, kvs, early, wo, head_gain, wh, bias):
    tokens, _ = rows.shape
    head = kvs[0].shape[1] // 2
    length = sum(kv.shape[0] for kv in kvs)
    tracks = wh.shape[1]
    return pl.pallas_call(
        functools.partial(block_kernel, len(kvs)),
        out_shape=(jax.ShapeDtypeStruct((tokens // 2, tracks), BF16),) * 2,
        in_specs=[SMEM] + [VMEM] * (6 + len(kvs) + len(early)),
        out_specs=(VMEM, VMEM),
        scratch_shapes=[
            pltpu.VMEM((length, queries.shape[1]), BF16),
            pltpu.VMEM((length, head), BF16),
            pltpu.VMEM((tokens, wo.shape[0]), BF16),
            pltpu.VMEM((tokens, tracks), BF16),
        ],
        compiler_params=pltpu.CompilerParams(vmem_limit_bytes=28 << 20),
        cost_estimate=pl.CostEstimate(
            flops=2 * tokens * (wo.size + wh.size) + 4 * queries.size * (length + sum(part.shape[0] for part in early)),
            bytes_accessed=2 * (wo.size + wh.size),
            transcendentals=queries.shape[0] * length,
        ),
        name="transform",
    )(core, queries, rows, *kvs, *early, wo, head_gain, wh, bias)


def combine_kernel(core_ref, keep_ref, got_ref, perm_ref, out_ref, forward_ref, reverse_ref):
    forward_here = core_ref[0] == 0
    keep = keep_ref[...].astype(F32)
    got = got_ref[...].astype(F32)
    forward_ref[...] = jnp.where(forward_here, keep, got)
    reverse_ref[...] = jnp.where(forward_here, got, keep)
    tracks = perm_ref.shape[0]
    tokens = keep_ref.shape[0]
    order = perm_ref[...].reshape(1, -1)
    lanes = 128
    group = 8
    for at in range(0, tracks, lanes):
        perm = jnp.broadcast_to(order[:, at : at + lanes], (group, lanes))
        within = perm & (lanes - 1)
        tile = perm >> 7
        inside = [tile == number for number in range(1, tracks // lanes)]
        for row in range(0, tokens, group):
            rows = slice(row, row + group)
            picked = jnp.take_along_axis(reverse_ref[rows, :lanes], within, axis=1)
            for number, here in enumerate(inside, 1):
                source = reverse_ref[rows, number * lanes : (number + 1) * lanes]
                picked = jnp.where(here, jnp.take_along_axis(source, within, axis=1), picked)
            out_ref[rows, at : at + lanes] = 0.5 * (forward_ref[rows, at : at + lanes] + picked)


def combine(core, keep, got, perm):
    return pl.pallas_call(
        combine_kernel,
        out_shape=jax.ShapeDtypeStruct(keep.shape, F32),
        in_specs=[SMEM] + [VMEM] * 3,
        out_specs=VMEM,
        scratch_shapes=[pltpu.VMEM(keep.shape, F32)] * 2,
        compiler_params=pltpu.CompilerParams(vmem_limit_bytes=16 << 20),
        name="combine",
    )(core, keep, got, perm)


def gathered(kv):
    count = lax.axis_size("tok")
    if count != 16:
        mask = 2
        while mask < count:
            kv = jnp.concatenate([kv, exchange(kv, mask)], 0)
            mask *= 2
        return [], [kv]
    z2 = exchange(kv, 8)
    z1 = exchange(kv, 4)
    x = exchange(kv, 2)
    xz1 = exchange(z1, 2)
    z3 = exchange(z2, 4)
    xz2 = exchange(z2, 2)
    xz3 = exchange(z3, 2)
    return [kv, x, z1, xz1, z2, z3], [xz2, xz3]


def per_device(
    hidden,
    base_ids,
    attn_gain,
    q_weight,
    kv_weight,
    out_weight,
    head_gain,
    head_weight,
    head_bias,
    track_perm,
):
    count = lax.axis_size("tok")
    core = (lax.axis_index("tok") & 1).astype(jnp.int32).reshape(1)
    got = exchange(hidden, 1)
    got_ids = exchange(base_ids, 1)
    own, gain, own_ids, kv_weight = fetch([hidden, attn_gain, base_ids, kv_weight])
    kv, turned = project(core, got, got_ids, own, own_ids, gain, kv_weight)
    mirrored = exchange(turned, count - 2)
    early, late = gathered(kv)
    wh, bias = fetch([head_weight, head_bias], after=kv)
    wq, wo, head_gain = fetch([q_weight, out_weight, head_gain], after=bias)
    passed = exchange(mirrored, 1)
    if early:
        early = packed(early)
    queries, rows = query(core, own, got, mirrored, passed, gain, wq, kv.shape[1] // 2)
    keep, send = transform(core, queries, rows, late, early, wo, head_gain, wh, bias)
    return combine(core, keep, exchange(send, 1), track_perm)


def solution(mesh):
    placed = (P("grp", "tok", None), P("grp", "tok"), P(), P(), P(), P(), P(), P(), P(), P())
    return jax.shard_map(per_device, mesh=mesh, in_specs=placed, out_specs=P(("grp", "tok"), None), check_vma=False)
```

time: 37.8 us -> 38.3 us (1.013)
  waiting for transfers between devices: 8.25 us -> 15.2 us
  starting transfers between devices: 16.9 us -> 10.8 us
    ppermute x12, waiting for transfers between devices: 8.25 us -> 15.2 us  [exchange(): return lax.ppermute(value, 'tok', [(s, s ^ mask) for s in range(count)])]
    ppermute x12, starting transfers between devices: 16.9 us -> 10.8 us  [exchange(): return lax.ppermute(value, 'tok', [(s, s ^ mask) for s in range(count)])]
    pallas_call x1, Pallas kernels: 3.32 us -> 2.87 us  [transform(): pl.pallas_call(functools.partial(block_kernel, len(kvs)), out_shape=(jax....]
  transfers between devices with their start and end apart: 12 -> 12, of which waited for: 8 -> 5; matrix products, arithmetic and copies ran while one was open for 0% -> 0% of each run, Pallas kernels for 20% -> 19%
where the time goes in v3:
time: 38.3 us; the launch traced here: 38.2 us
  waiting for transfers between devices  15.2 us (40%)
  Pallas kernels  12.1 us (32%)
  starting transfers between devices  10.8 us (28%)
    ppermute x12, waiting for transfers between devices, exchange(): return lax.ppermute(value, 'tok', [(s, s ^ mask) for s in range(count)])  15.2 us
    ppermute x12, starting transfers between devices, exchange(): return lax.ppermute(value, 'tok', [(s, s ^ mask) for s in range(count)])  10.8 us
    pallas_call x3, Pallas kernels, fetch(): pl.pallas_call(functools.partial(fetch_kernel, len(values)), out_shape=[j...  6.23 us
    pallas_call x1, Pallas kernels, transform(): pl.pallas_call(functools.partial(block_kernel, len(kvs)), out_shape=(jax....  2.87 us
    pallas_call x1, Pallas kernels, combine(): pl.pallas_call(combine_kernel, out_shape=jax.ShapeDtypeStruct(keep.shape,...  1.46 us
  transfers between devices with their start and end apart: 12, of which 5 were waited for; matrix products, arithmetic and copies ran while one was open for 0% of the time, Pallas kernels for 19%

profile of v3, /device:TPU:0, one launch (start us, length us, event | category | flops | bytes accessed | tf_op | source)
XLA Modules:
  0.0 38.2 jit_solution(12076077004882530548)
XLA Ops:
  0.0 0.5 %collective-permute-start = (bf16[2,64,1536]{2,1,0:T(8,128)(2,1)}, bf16[2,64,1536]{2,1,0:T(8,128)(2,1)S(1)}, u32[]{:S(2)}, u32[]{:S(2)}) collective-permute-start(bf16[2,64,1536]{2,1,0:T(8,128)(2,1)} %refs_0_.3), channel_id=1, source_target_pairs={{0,1},{1,0},{2,3},{3,2},{4,5},{5,4},{6,7},{7,6},{8,9},{9,8},{10,11... | collective-permute-start | bytes 1179656 | tf_op jit(solution)/shard_map/ppermute | solution.py:25
  0.5 0.0 collective-permute-start.1
  0.5 1.5 %fetch.3 = (bf16[2,64,1536]{2,1,0:T(8,128)(2,1)S(1)}, bf16[1536]{0:T(1024)(128)(2,1)S(1)}, s32[2,64]{1,0:T(2,128)S(1)}, bf16[1536,384]{1,0:T(8,128)(2,1)S(1)}) custom-call(bf16[2,64,1536]{2,1,0:T(8,128)(2,1)} %refs_0_.3, bf16[1536]{0:T(1024)(128)(2,1)} %refs_1_.3, s32[2,64]{1,0:T(2,128)} %refs_2_.2, bf16[1536,384]{1,0:T(8,128)(2,1)} %refs_3_.1), custom_call_target="tpu_custom_call" | custom-call | bytes 1576192 | tf_op jit(solution)/shard_map/fetch/pallas_call | solution.py:47
  2.0 0.1 collective-permute-done.1.got_ids_ref
  2.1 0.0 collective-permute-done.got_ref
  2.1 0.5 %project.1 = (bf16[128,384]{1,0:T(8,128)(2,1)S(1)}, bf16[64,1536]{1,0:T(8,128)(2,1)S(1)}) custom-call(s32[1]{0:T(128)} %bitcast.core_ref, bf16[2,64,1536]{2,1,0:T(8,128)(2,1)S(1)} %collective-permute-done.got_ref, s32[2,64]{1,0:T(2,128)S(1)} %collective-permute-done.1.got_ids_ref, bf16[2,64,1536]{2,1,0:T(8,128)(2,1)S(1)} %get-tuple-element.22.own_ref, ...), custom_call_target="tpu_custom_call" | custom-call | flops 150994944 | bytes 1179648 | tf_op jit(solution)/shard_map/project/pallas_call | solution.py:86
  2.6 6.0 %collective-permute-start.2 = (bf16[64,1536]{1,0:T(8,128)(2,1)S(1)}, bf16[64,1536]{1,0:T(8,128)(2,1)S(1)}, u32[]{:S(2)}, u32[]{:S(2)}) collective-permute-start(bf16[64,1536]{1,0:T(8,128)(2,1)S(1)} %get-tuple-element.26), channel_id=1, source_target_pairs={{0,14},{1,15},{2,12},{3,13},{4,10},{5,11},{6,8},{7,9},{8,6},{9,7},... | collective-permute-start | bytes 589832 | tf_op jit(solution)/shard_map/ppermute | solution.py:25
  8.6 0.0 collective-permute-start.4
  8.6 0.8 %collective-permute-start.9 = (bf16[128,384]{1,0:T(8,128)(2,1)S(1)}, bf16[128,384]{1,0:T(8,128)(2,1)S(1)}, u32[]{:S(2)}, u32[]{:S(2)}) collective-permute-start(bf16[128,384]{1,0:T(8,128)(2,1)S(1)} %get-tuple-element.27.refs_2_.refs_0_), channel_id=1, source_target_pairs={{0,4},{1,5},{2,6},{3,7},{4,0},{5,1},{6,2},{7,3},{8,12},{9,13},{10,... | collective-permute-start | bytes 294920 | tf_op jit(solution)/shard_map/ppermute | solution.py:25
  9.4 5.1 %collective-permute-done.2.mirrored_ref = bf16[64,1536]{1,0:T(8,128)(2,1)S(1)} collective-permute-done((bf16[64,1536]{1,0:T(8,128)(2,1)S(1)}, bf16[64,1536]{1,0:T(8,128)(2,1)S(1)}, u32[]{:S(2)}, u32[]{:S(2)}) %collective-permute-start.2) | collective-permute-done | bytes 196640 | tf_op jit(solution)/shard_map/ppermute | solution.py:25
  14.5 0.0 collective-permute-start.3
  14.5 6.8 %collective-permute-done.4.refs_4_ = bf16[128,384]{1,0:T(8,128)(2,1)S(1)} collective-permute-done((bf16[128,384]{1,0:T(8,128)(2,1)S(1)}, bf16[128,384]{1,0:T(8,128)(2,1)S(1)}, u32[]{:S(2)}, u32[]{:S(2)}) %collective-permute-start.4) | collective-permute-done | bytes 98336 | tf_op jit(solution)/shard_map/ppermute | solution.py:25
  21.3 0.0 collective-permute-start.6
  21.3 0.8 %collective-permute-start.8 = (bf16[128,384]{1,0:T(8,128)(2,1)S(1)}, bf16[128,384]{1,0:T(8,128)(2,1)S(1)}, u32[]{:S(2)}, u32[]{:S(2)}) collective-permute-start(bf16[128,384]{1,0:T(8,128)(2,1)S(1)} %get-tuple-element.27.refs_2_.refs_0_), channel_id=1, source_target_pairs={{0,2},{1,3},{2,0},{3,1},{4,6},{5,7},{6,4},{7,5},{8,10},{9,11},{10,... | collective-permute-start | bytes 294920 | tf_op jit(solution)/shard_map/ppermute | solution.py:25
  22.1 0.0 collective-permute-done.9.refs_2_
  22.1 1.2 %collective-permute-start.10 = (bf16[128,384]{1,0:T(8,128)(2,1)S(1)}, bf16[128,384]{1,0:T(8,128)(2,1)S(1)}, u32[]{:S(2)}, u32[]{:S(2)}) collective-permute-start(bf16[128,384]{1,0:T(8,128)(2,1)S(1)} %collective-permute-done.9.refs_2_), channel_id=1, source_target_pairs={{0,2},{1,3},{2,0},{3,1},{4,6},{5,7},{6,4},{7,5},{8,10},{9,11},{10,... | collective-permute-start | bytes 294920 | tf_op jit(solution)/shard_map/ppermute | solution.py:25
  23.3 0.8 %collective-permute-start.5 = (bf16[128,384]{1,0:T(8,128)(2,1)S(1)}, bf16[128,384]{1,0:T(8,128)(2,1)S(1)}, u32[]{:S(2)}, u32[]{:S(2)}) collective-permute-start(bf16[128,384]{1,0:T(8,128)(2,1)S(1)} %collective-permute-done.4.refs_4_), channel_id=1, source_target_pairs={{0,2},{1,3},{2,0},{3,1},{4,6},{5,7},{6,4},{7,5},{8,10},{9,11},{10,... | collective-permute-start | bytes 294920 | tf_op jit(solution)/shard_map/ppermute | solution.py:25
  24.1 1.8 %collective-permute-done.6.refs_5_ = bf16[128,384]{1,0:T(8,128)(2,1)S(1)} collective-permute-done((bf16[128,384]{1,0:T(8,128)(2,1)S(1)}, bf16[128,384]{1,0:T(8,128)(2,1)S(1)}, u32[]{:S(2)}, u32[]{:S(2)}) %collective-permute-start.6) | collective-permute-done | bytes 98336 | tf_op jit(solution)/shard_map/ppermute | solution.py:25
  25.9 0.5 %collective-permute-start.7 = (bf16[128,384]{1,0:T(8,128)(2,1)S(1)}, bf16[128,384]{1,0:T(8,128)(2,1)S(1)}, u32[]{:S(2)}, u32[]{:S(2)}) collective-permute-start(bf16[128,384]{1,0:T(8,128)(2,1)S(1)} %collective-permute-done.6.refs_5_), channel_id=1, source_target_pairs={{0,2},{1,3},{2,0},{3,1},{4,6},{5,7},{6,4},{7,5},{8,10},{9,11},{10,... | collective-permute-start | bytes 294920 | tf_op jit(solution)/shard_map/ppermute | solution.py:25
  26.5 2.4 %fetch.4 = (bf16[1536,1536]{1,0:T(8,128)(2,1)S(1)}, f32[1536]{0:T(1024)S(1)}) custom-call(bf16[1536,1536]{1,0:T(8,128)(2,1)} %refs_0_.4, f32[1536]{0:T(1024)} %refs_1_.4, bf16[128,384]{1,0:T(8,128)(2,1)S(1)} %get-tuple-element.27.refs_2_.refs_0_), custom_call_target="tpu_custom_call" | custom-call | bytes 4721664 | tf_op jit(solution)/shard_map/fetch/pallas_call | solution.py:47
  28.8 2.4 %fetch.5 = (bf16[1536,768]{1,0:T(8,128)(2,1)S(1)}, bf16[768,1536]{1,0:T(8,128)(2,1)S(1)}, bf16[1536]{0:T(1024)(128)(2,1)S(1)}) custom-call(bf16[1536,768]{1,0:T(8,128)(2,1)} %refs_0_.5, bf16[768,1536]{1,0:T(8,128)(2,1)} %refs_1_.5, bf16[1536]{0:T(1024)(128)(2,1)} %refs_2_.3, f32[1536]{0:T(1024)S(1)} %get-tuple-element.28.refs_3_.refs_7_), custom_call_target="tpu_custom_call" | custom-call | bytes 4721664 | tf_op jit(solution)/shard_map/fetch/pallas_call | solution.py:47
  31.2 0.0 collective-permute-done.8.refs_1_
  31.2 0.0 collective-permute-done.10.refs_3_
  31.3 0.3 packed.1
  31.5 0.0 collective-permute-done.3.passed_ref
  31.6 0.8 %query.1 = (bf16[512,256]{1,0:T(8,128)(2,1)S(1)}, f32[128,1536]{1,0:T(8,128)S(1)}) custom-call(s32[1]{0:T(128)} %bitcast.core_ref, bf16[2,64,1536]{2,1,0:T(8,128)(2,1)S(1)} %get-tuple-element.22.own_ref, bf16[2,64,1536]{2,1,0:T(8,128)(2,1)S(1)} %collective-permute-done.got_ref, bf16[64,1536]{1,0:T(8,128)(2,1)S(1)} %collective-permute-done.2.mirrored_ref, ...), custom_call_target="tpu_custom_call" | custom-call | flops 301989888 | bytes 2359296 | tf_op jit(solution)/shard_map/query/pallas_call | solution.py:196
  32.3 0.0 collective-permute-done.5.refs_0_
  32.3 0.0 collective-permute-done.7.refs_1_
  32.3 0.0 copy-start
  32.3 2.9 %transform.1 = (bf16[64,1536]{1,0:T(8,128)(2,1)S(1)}, bf16[64,1536]{1,0:T(8,128)(2,1)S(1)}) custom-call(s32[1]{0:T(128)} %bitcast.core_ref, bf16[512,256]{1,0:T(8,128)(2,1)S(1)} %get-tuple-element.30.query_ref, f32[128,1536]{1,0:T(8,128)S(1)} %get-tuple-element.31.rows_ref, bf16[128,384]{1,0:T(8,128)(2,1)S(1)} %collective-permute-done.5.refs_0_, ...), custom_call_target="tpu_custom_call" | custom-call | flops 1845493760 | bytes 7077888 | tf_op jit(solution)/shard_map/transform/pallas_call | solution.py:251
  35.2 0.1 collective-permute-start.11
  35.3 1.4 %collective-permute-done.11.got_ref = bf16[64,1536]{1,0:T(8,128)(2,1)S(1)} collective-permute-done((bf16[64,1536]{1,0:T(8,128)(2,1)S(1)}, bf16[64,1536]{1,0:T(8,128)(2,1)S(1)}, u32[]{:S(2)}, u32[]{:S(2)}) %collective-permute-start.11) | collective-permute-done | bytes 196640 | tf_op jit(solution)/shard_map/ppermute | solution.py:25
  36.7 0.0 copy-done
  36.7 1.5 %combine.1 = f32[64,1536]{1,0:T(8,128)} custom-call(s32[1]{0:T(128)} %bitcast.core_ref, bf16[64,1536]{1,0:T(8,128)(2,1)S(1)} %get-tuple-element.37.keep_ref, bf16[64,1536]{1,0:T(8,128)(2,1)S(1)} %collective-permute-done.11.got_ref, s32[1536]{0:T(1024)S(1)} %copy-done), custom_call_target="tpu_custom_call" | custom-call | tf_op jit(solution)/shard_map/combine/pallas_call | solution.py:298
Async XLA Ops:
  0.0 2.1 %collective-permute-start = (bf16[2,64,1536]{2,1,0:T(8,128)(2,1)}, bf16[2,64,1536]{2,1,0:T(8,128)(2,1)S(1)}, u32[]{:S(2)}, u32[]{:S(2)}) collective-permute-start(bf16[2,64,1536]{2,1,0:T(8,128)(2,1)} %refs_0_.3), channel_id=1, source_target_pairs={{0,1},{1,0},{2,3},{3,2},{4,5},{5,4},{6,7},{7,6},{8,9},{9,8},{10,11... | collective-permute-start | bytes 1179656 | tf_op jit(solution)/shard_map/ppermute | solution.py:25
  0.5 1.6 %collective-permute-start.1 = (s32[2,64]{1,0:T(2,128)}, s32[2,64]{1,0:T(2,128)S(1)}, u32[]{:S(2)}, u32[]{:S(2)}) collective-permute-start(s32[2,64]{1,0:T(2,128)} %refs_2_.2), channel_id=1, source_target_pairs={{0,1},{1,0},{2,3},{3,2},{4,5},{5,4},{6,7},{7,6},{8,9},{9,8},{10,11... | collective-permute-start | bytes 1544 | tf_op jit(solution)/shard_map/ppermute | solution.py:25
  2.6 11.9 %collective-permute-start.2 = (bf16[64,1536]{1,0:T(8,128)(2,1)S(1)}, bf16[64,1536]{1,0:T(8,128)(2,1)S(1)}, u32[]{:S(2)}, u32[]{:S(2)}) collective-permute-start(bf16[64,1536]{1,0:T(8,128)(2,1)S(1)} %get-tuple-element.26), channel_id=1, source_target_pairs={{0,14},{1,15},{2,12},{3,13},{4,10},{5,11},{6,8},{7,9},{8,6},{9,7},... | collective-permute-start | bytes 589832 | tf_op jit(solution)/shard_map/ppermute | solution.py:25
  8.6 12.7 %collective-permute-start.4 = (bf16[128,384]{1,0:T(8,128)(2,1)S(1)}, bf16[128,384]{1,0:T(8,128)(2,1)S(1)}, u32[]{:S(2)}, u32[]{:S(2)}) collective-permute-start(bf16[128,384]{1,0:T(8,128)(2,1)S(1)} %get-tuple-element.27.refs_2_.refs_0_), channel_id=1, source_target_pairs={{0,8},{1,9},{2,10},{3,11},{4,12},{5,13},{6,14},{7,15},{8,0},{9,1},... | collective-permute-start | bytes 294920 | tf_op jit(solution)/shard_map/ppermute | solution.py:25
  8.6 13.5 %collective-permute-start.9 = (bf16[128,384]{1,0:T(8,128)(2,1)S(1)}, bf16[128,384]{1,0:T(8,128)(2,1)S(1)}, u32[]{:S(2)}, u32[]{:S(2)}) collective-permute-start(bf16[128,384]{1,0:T(8,128)(2,1)S(1)} %get-tuple-element.27.refs_2_.refs_0_), channel_id=1, source_target_pairs={{0,4},{1,5},{2,6},{3,7},{4,0},{5,1},{6,2},{7,3},{8,12},{9,13},{10,... | collective-permute-start | bytes 294920 | tf_op jit(solution)/shard_map/ppermute | solution.py:25
  14.5 17.1 %collective-permute-start.3 = (bf16[64,1536]{1,0:T(8,128)(2,1)S(1)}, bf16[64,1536]{1,0:T(8,128)(2,1)S(1)}, u32[]{:S(2)}, u32[]{:S(2)}) collective-permute-start(bf16[64,1536]{1,0:T(8,128)(2,1)S(1)} %collective-permute-done.2.mirrored_ref), channel_id=1, source_target_pairs={{0,1},{1,0},{2,3},{3,2},{4,5},{5,4},{6,7},{7,6},{8,9},{9,8},{10,11... | collective-permute-start | bytes 589832 | tf_op jit(solution)/shard_map/ppermute | solution.py:25
  21.3 4.6 %collective-permute-start.6 = (bf16[128,384]{1,0:T(8,128)(2,1)S(1)}, bf16[128,384]{1,0:T(8,128)(2,1)S(1)}, u32[]{:S(2)}, u32[]{:S(2)}) collective-permute-start(bf16[128,384]{1,0:T(8,128)(2,1)S(1)} %collective-permute-done.4.refs_4_), channel_id=1, source_target_pairs={{0,4},{1,5},{2,6},{3,7},{4,0},{5,1},{6,2},{7,3},{8,12},{9,13},{10,... | collective-permute-start | bytes 294920 | tf_op jit(solution)/shard_map/ppermute | solution.py:25
  21.3 9.9 %collective-permute-start.8 = (bf16[128,384]{1,0:T(8,128)(2,1)S(1)}, bf16[128,384]{1,0:T(8,128)(2,1)S(1)}, u32[]{:S(2)}, u32[]{:S(2)}) collective-permute-start(bf16[128,384]{1,0:T(8,128)(2,1)S(1)} %get-tuple-element.27.refs_2_.refs_0_), channel_id=1, source_target_pairs={{0,2},{1,3},{2,0},{3,1},{4,6},{5,7},{6,4},{7,5},{8,10},{9,11},{10,... | collective-permute-start | bytes 294920 | tf_op jit(solution)/shard_map/ppermute | solution.py:25
  22.1 9.1 %collective-permute-start.10 = (bf16[128,384]{1,0:T(8,128)(2,1)S(1)}, bf16[128,384]{1,0:T(8,128)(2,1)S(1)}, u32[]{:S(2)}, u32[]{:S(2)}) collective-permute-start(bf16[128,384]{1,0:T(8,128)(2,1)S(1)} %collective-permute-done.9.refs_2_), channel_id=1, source_target_pairs={{0,2},{1,3},{2,0},{3,1},{4,6},{5,7},{6,4},{7,5},{8,10},{9,11},{10,... | collective-permute-start | bytes 294920 | tf_op jit(solution)/shard_map/ppermute | solution.py:25
  23.3 9.0 %collective-permute-start.5 = (bf16[128,384]{1,0:T(8,128)(2,1)S(1)}, bf16[128,384]{1,0:T(8,128)(2,1)S(1)}, u32[]{:S(2)}, u32[]{:S(2)}) collective-permute-start(bf16[128,384]{1,0:T(8,128)(2,1)S(1)} %collective-permute-done.4.refs_4_), channel_id=1, source_target_pairs={{0,2},{1,3},{2,0},{3,1},{4,6},{5,7},{6,4},{7,5},{8,10},{9,11},{10,... | collective-permute-start | bytes 294920 | tf_op jit(solution)/shard_map/ppermute | solution.py:25
  25.9 6.4 %collective-permute-start.7 = (bf16[128,384]{1,0:T(8,128)(2,1)S(1)}, bf16[128,384]{1,0:T(8,128)(2,1)S(1)}, u32[]{:S(2)}, u32[]{:S(2)}) collective-permute-start(bf16[128,384]{1,0:T(8,128)(2,1)S(1)} %collective-permute-done.6.refs_5_), channel_id=1, source_target_pairs={{0,2},{1,3},{2,0},{3,1},{4,6},{5,7},{6,4},{7,5},{8,10},{9,11},{10,... | collective-permute-start | bytes 294920 | tf_op jit(solution)/shard_map/ppermute | solution.py:25
  32.3 4.4 %copy-start = (s32[1536]{0:T(1024)S(1)}, s32[1536]{0:T(1024)}, u32[]{:S(2)}) copy-start(s32[1536]{0:T(1024)} %perm_ref.1) | copy-start | bytes 18436
  35.2 1.5 %collective-permute-start.11 = (bf16[64,1536]{1,0:T(8,128)(2,1)S(1)}, bf16[64,1536]{1,0:T(8,128)(2,1)S(1)}, u32[]{:S(2)}, u32[]{:S(2)}) collective-permute-start(bf16[64,1536]{1,0:T(8,128)(2,1)S(1)} %get-tuple-element.38), channel_id=1, source_target_pairs={{0,1},{1,0},{2,3},{3,2},{4,5},{5,4},{6,7},{7,6},{8,9},{9,8},{10,11... | collective-permute-start | bytes 589832 | tf_op jit(solution)/shard_map/ppermute | solution.py:25

commit v4 on v3

--- a/solution.py
+++ b/solution.py
@@ -103,11 +103,13 @@
     rate = math.log2(math.e) / math.sqrt(head)
     chunk = 1024
 
-    def step(parts, state):
-        scores = [
-            lax.dot_general(queries, keys, (((1,), (1,)), ((), ())), preferred_element_type=F32)
+    def score(block, parts):
+        return [
+            lax.dot_general(block, keys, (((1,), (1,)), ((), ())), preferred_element_type=F32)
             for keys, _ in parts
         ]
+
+    def weigh(scores, parts, state):
         maxima = functools.reduce(jnp.maximum, [jnp.max(part, -1, keepdims=True) for part in scores])
         if state is not None:
             maxima = jnp.maximum(maxima, state[0])
@@ -124,12 +126,15 @@
         return maxima, totals, summed
 
     if sum(keys.shape[0] for keys, _ in segments) <= chunk:
-        return step([(keys[...], values[...]) for keys, values in segments], None)
+        parts = [(keys[...], values[...]) for keys, values in segments]
+        return [weigh(products, parts, None) for products in [score(block, parts) for block in queries]]
     keys, values = segments[0]
 
-    def one(position, state):
+    def one(position, states):
         at = pl.ds(pl.multiple_of(position * chunk, chunk), chunk)
-        return step([(keys[at, :], values[at, :])], state)
+        parts = [(keys[at, :], values[at, :])]
+        states = [None] * len(queries) if states is None else states
+        return [weigh(score(block, parts), parts, state) for block, state in zip(queries, states)]
 
     return lax.fori_loop(1, keys.shape[0] // chunk, one, one(0, None))
 
@@ -221,13 +226,11 @@
     segments = ([early] if early else []) + [(keys, values)]
     heads = query_ref.shape[0] // tokens
     group = 2 if heads % 2 == 0 else 1
-    for first in range(0, heads, group):
-        _, totals, summed = attend(
-            query_ref[pl.ds(first * tokens, group * tokens), :], segments, head
-        )
-        result = (summed / totals).astype(BF16)
+    blocks = [query_ref[pl.ds(first * tokens, group * tokens), :] for first in range(0, heads, group)]
+    for first, (_, totals, summed) in enumerate(attend(blocks, segments, head)):
+        result = (summed * (1.0 / totals)).astype(BF16)
         for number in range(group):
-            at = (first + number) * head
+            at = (first * group + number) * head
             attended[:, at : at + head] = result[number * tokens : (number + 1) * tokens]
     summed = rows_ref[...] + jnp.dot(attended[...], wo[...], preferred_element_type=F32)
     normed_out = normalize(summed, head_gain_ref[...].astype(F32).reshape(1, -1))

time: 38.3 us -> 38.2 us (level)
  no operation moved by 1% of the time
where the time goes in v4:
time: 38.2 us; the launch traced here: 38 us
  waiting for transfers between devices  15.2 us (40%)
  Pallas kernels  11.9 us (31%)
  starting transfers between devices  10.8 us (28%)
    ppermute x12, waiting for transfers between devices, exchange(): return lax.ppermute(value, 'tok', [(s, s ^ mask) for s in range(count)])  15.2 us
    ppermute x12, starting transfers between devices, exchange(): return lax.ppermute(value, 'tok', [(s, s ^ mask) for s in range(count)])  10.8 us
    pallas_call x3, Pallas kernels, fetch(): pl.pallas_call(functools.partial(fetch_kernel, len(values)), out_shape=[j...  6.23 us
    pallas_call x1, Pallas kernels, transform(): pl.pallas_call(functools.partial(block_kernel, len(kvs)), out_shape=(jax....  2.7 us
    pallas_call x1, Pallas kernels, combine(): pl.pallas_call(combine_kernel, out_shape=jax.ShapeDtypeStruct(keep.shape,...  1.46 us
  transfers between devices with their start and end apart: 12, of which 5 were waited for; matrix products, arithmetic and copies ran while one was open for 0% of the time, Pallas kernels for 19%

profile of v4, /device:TPU:0, one launch (start us, length us, event | category | flops | bytes accessed | tf_op | source)
XLA Modules:
  0.0 38.0 jit_solution(5998651121621938123)
XLA Ops:
  0.0 0.5 %collective-permute-start = (bf16[2,64,1536]{2,1,0:T(8,128)(2,1)}, bf16[2,64,1536]{2,1,0:T(8,128)(2,1)S(1)}, u32[]{:S(2)}, u32[]{:S(2)}) collective-permute-start(bf16[2,64,1536]{2,1,0:T(8,128)(2,1)} %refs_0_.3), channel_id=1, source_target_pairs={{0,1},{1,0},{2,3},{3,2},{4,5},{5,4},{6,7},{7,6},{8,9},{9,8},{10,11... | collective-permute-start | bytes 1179656 | tf_op jit(solution)/shard_map/ppermute | solution.py:25
  0.5 0.0 collective-permute-start.1
  0.5 1.5 %fetch.3 = (bf16[2,64,1536]{2,1,0:T(8,128)(2,1)S(1)}, bf16[1536]{0:T(1024)(128)(2,1)S(1)}, s32[2,64]{1,0:T(2,128)S(1)}, bf16[1536,384]{1,0:T(8,128)(2,1)S(1)}) custom-call(bf16[2,64,1536]{2,1,0:T(8,128)(2,1)} %refs_0_.3, bf16[1536]{0:T(1024)(128)(2,1)} %refs_1_.3, s32[2,64]{1,0:T(2,128)} %refs_2_.2, bf16[1536,384]{1,0:T(8,128)(2,1)} %refs_3_.1), custom_call_target="tpu_custom_call" | custom-call | bytes 1576192 | tf_op jit(solution)/shard_map/fetch/pallas_call | solution.py:47
  2.0 0.1 collective-permute-done.1.got_ids_ref
  2.1 0.0 collective-permute-done.got_ref
  2.1 0.5 %project.1 = (bf16[128,384]{1,0:T(8,128)(2,1)S(1)}, bf16[64,1536]{1,0:T(8,128)(2,1)S(1)}) custom-call(s32[1]{0:T(128)} %bitcast.core_ref, bf16[2,64,1536]{2,1,0:T(8,128)(2,1)S(1)} %collective-permute-done.got_ref, s32[2,64]{1,0:T(2,128)S(1)} %collective-permute-done.1.got_ids_ref, bf16[2,64,1536]{2,1,0:T(8,128)(2,1)S(1)} %get-tuple-element.22.own_ref, ...), custom_call_target="tpu_custom_call" | custom-call | flops 150994944 | bytes 1179648 | tf_op jit(solution)/shard_map/project/pallas_call | solution.py:86
  2.6 6.0 %collective-permute-start.2 = (bf16[64,1536]{1,0:T(8,128)(2,1)S(1)}, bf16[64,1536]{1,0:T(8,128)(2,1)S(1)}, u32[]{:S(2)}, u32[]{:S(2)}) collective-permute-start(bf16[64,1536]{1,0:T(8,128)(2,1)S(1)} %get-tuple-element.26), channel_id=1, source_target_pairs={{0,14},{1,15},{2,12},{3,13},{4,10},{5,11},{6,8},{7,9},{8,6},{9,7},... | collective-permute-start | bytes 589832 | tf_op jit(solution)/shard_map/ppermute | solution.py:25
  8.6 0.0 collective-permute-start.4
  8.6 0.8 %collective-permute-start.9 = (bf16[128,384]{1,0:T(8,128)(2,1)S(1)}, bf16[128,384]{1,0:T(8,128)(2,1)S(1)}, u32[]{:S(2)}, u32[]{:S(2)}) collective-permute-start(bf16[128,384]{1,0:T(8,128)(2,1)S(1)} %get-tuple-element.27.refs_2_.refs_0_), channel_id=1, source_target_pairs={{0,4},{1,5},{2,6},{3,7},{4,0},{5,1},{6,2},{7,3},{8,12},{9,13},{10,... | collective-permute-start | bytes 294920 | tf_op jit(solution)/shard_map/ppermute | solution.py:25
  9.4 5.1 %collective-permute-done.2.mirrored_ref = bf16[64,1536]{1,0:T(8,128)(2,1)S(1)} collective-permute-done((bf16[64,1536]{1,0:T(8,128)(2,1)S(1)}, bf16[64,1536]{1,0:T(8,128)(2,1)S(1)}, u32[]{:S(2)}, u32[]{:S(2)}) %collective-permute-start.2) | collective-permute-done | bytes 196640 | tf_op jit(solution)/shard_map/ppermute | solution.py:25
  14.5 0.0 collective-permute-start.3
  14.5 6.8 %collective-permute-done.4.refs_4_ = bf16[128,384]{1,0:T(8,128)(2,1)S(1)} collective-permute-done((bf16[128,384]{1,0:T(8,128)(2,1)S(1)}, bf16[128,384]{1,0:T(8,128)(2,1)S(1)}, u32[]{:S(2)}, u32[]{:S(2)}) %collective-permute-start.4) | collective-permute-done | bytes 98336 | tf_op jit(solution)/shard_map/ppermute | solution.py:25
  21.3 0.0 collective-permute-start.6
  21.3 0.8 %collective-permute-start.8 = (bf16[128,384]{1,0:T(8,128)(2,1)S(1)}, bf16[128,384]{1,0:T(8,128)(2,1)S(1)}, u32[]{:S(2)}, u32[]{:S(2)}) collective-permute-start(bf16[128,384]{1,0:T(8,128)(2,1)S(1)} %get-tuple-element.27.refs_2_.refs_0_), channel_id=1, source_target_pairs={{0,2},{1,3},{2,0},{3,1},{4,6},{5,7},{6,4},{7,5},{8,10},{9,11},{10,... | collective-permute-start | bytes 294920 | tf_op jit(solution)/shard_map/ppermute | solution.py:25
  22.1 0.0 collective-permute-done.9.refs_2_
  22.1 1.2 %collective-permute-start.10 = (bf16[128,384]{1,0:T(8,128)(2,1)S(1)}, bf16[128,384]{1,0:T(8,128)(2,1)S(1)}, u32[]{:S(2)}, u32[]{:S(2)}) collective-permute-start(bf16[128,384]{1,0:T(8,128)(2,1)S(1)} %collective-permute-done.9.refs_2_), channel_id=1, source_target_pairs={{0,2},{1,3},{2,0},{3,1},{4,6},{5,7},{6,4},{7,5},{8,10},{9,11},{10,... | collective-permute-start | bytes 294920 | tf_op jit(solution)/shard_map/ppermute | solution.py:25
  23.3 0.8 %collective-permute-start.5 = (bf16[128,384]{1,0:T(8,128)(2,1)S(1)}, bf16[128,384]{1,0:T(8,128)(2,1)S(1)}, u32[]{:S(2)}, u32[]{:S(2)}) collective-permute-start(bf16[128,384]{1,0:T(8,128)(2,1)S(1)} %collective-permute-done.4.refs_4_), channel_id=1, source_target_pairs={{0,2},{1,3},{2,0},{3,1},{4,6},{5,7},{6,4},{7,5},{8,10},{9,11},{10,... | collective-permute-start | bytes 294920 | tf_op jit(solution)/shard_map/ppermute | solution.py:25
  24.1 1.8 %collective-permute-done.6.refs_5_ = bf16[128,384]{1,0:T(8,128)(2,1)S(1)} collective-permute-done((bf16[128,384]{1,0:T(8,128)(2,1)S(1)}, bf16[128,384]{1,0:T(8,128)(2,1)S(1)}, u32[]{:S(2)}, u32[]{:S(2)}) %collective-permute-start.6) | collective-permute-done | bytes 98336 | tf_op jit(solution)/shard_map/ppermute | solution.py:25
  25.9 0.5 %collective-permute-start.7 = (bf16[128,384]{1,0:T(8,128)(2,1)S(1)}, bf16[128,384]{1,0:T(8,128)(2,1)S(1)}, u32[]{:S(2)}, u32[]{:S(2)}) collective-permute-start(bf16[128,384]{1,0:T(8,128)(2,1)S(1)} %collective-permute-done.6.refs_5_), channel_id=1, source_target_pairs={{0,2},{1,3},{2,0},{3,1},{4,6},{5,7},{6,4},{7,5},{8,10},{9,11},{10,... | collective-permute-start | bytes 294920 | tf_op jit(solution)/shard_map/ppermute | solution.py:25
  26.5 2.4 %fetch.4 = (bf16[1536,1536]{1,0:T(8,128)(2,1)S(1)}, f32[1536]{0:T(1024)S(1)}) custom-call(bf16[1536,1536]{1,0:T(8,128)(2,1)} %refs_0_.4, f32[1536]{0:T(1024)} %refs_1_.4, bf16[128,384]{1,0:T(8,128)(2,1)S(1)} %get-tuple-element.27.refs_2_.refs_0_), custom_call_target="tpu_custom_call" | custom-call | bytes 4721664 | tf_op jit(solution)/shard_map/fetch/pallas_call | solution.py:47
  28.8 2.4 %fetch.5 = (bf16[1536,768]{1,0:T(8,128)(2,1)S(1)}, bf16[768,1536]{1,0:T(8,128)(2,1)S(1)}, bf16[1536]{0:T(1024)(128)(2,1)S(1)}) custom-call(bf16[1536,768]{1,0:T(8,128)(2,1)} %refs_0_.5, bf16[768,1536]{1,0:T(8,128)(2,1)} %refs_1_.5, bf16[1536]{0:T(1024)(128)(2,1)} %refs_2_.3, f32[1536]{0:T(1024)S(1)} %get-tuple-element.28.refs_3_.refs_7_), custom_call_target="tpu_custom_call" | custom-call | bytes 4721664 | tf_op jit(solution)/shard_map/fetch/pallas_call | solution.py:47
  31.2 0.0 collective-permute-done.8.refs_1_
  31.2 0.0 collective-permute-done.10.refs_3_
  31.3 0.3 packed.1
  31.5 0.0 collective-permute-done.3.passed_ref
  31.6 0.8 %query.1 = (bf16[512,256]{1,0:T(8,128)(2,1)S(1)}, f32[128,1536]{1,0:T(8,128)S(1)}) custom-call(s32[1]{0:T(128)} %bitcast.core_ref, bf16[2,64,1536]{2,1,0:T(8,128)(2,1)S(1)} %get-tuple-element.22.own_ref, bf16[2,64,1536]{2,1,0:T(8,128)(2,1)S(1)} %collective-permute-done.got_ref, bf16[64,1536]{1,0:T(8,128)(2,1)S(1)} %collective-permute-done.2.mirrored_ref, ...), custom_call_target="tpu_custom_call" | custom-call | flops 301989888 | bytes 2359296 | tf_op jit(solution)/shard_map/query/pallas_call | solution.py:201
  32.3 0.0 collective-permute-done.5.refs_0_
  32.3 0.0 collective-permute-done.7.refs_1_
  32.3 0.0 copy-start
  32.3 2.7 %transform.1 = (bf16[64,1536]{1,0:T(8,128)(2,1)S(1)}, bf16[64,1536]{1,0:T(8,128)(2,1)S(1)}) custom-call(s32[1]{0:T(128)} %bitcast.core_ref, bf16[512,256]{1,0:T(8,128)(2,1)S(1)} %get-tuple-element.30.query_ref, f32[128,1536]{1,0:T(8,128)S(1)} %get-tuple-element.31.rows_ref, bf16[128,384]{1,0:T(8,128)(2,1)S(1)} %collective-permute-done.5.refs_0_, ...), custom_call_target="tpu_custom_call" | custom-call | flops 1845493760 | bytes 7077888 | tf_op jit(solution)/shard_map/transform/pallas_call | solution.py:254
  35.1 0.1 collective-permute-start.11
  35.1 1.4 %collective-permute-done.11.got_ref = bf16[64,1536]{1,0:T(8,128)(2,1)S(1)} collective-permute-done((bf16[64,1536]{1,0:T(8,128)(2,1)S(1)}, bf16[64,1536]{1,0:T(8,128)(2,1)S(1)}, u32[]{:S(2)}, u32[]{:S(2)}) %collective-permute-start.11) | collective-permute-done | bytes 196640 | tf_op jit(solution)/shard_map/ppermute | solution.py:25
  36.6 0.0 copy-done
  36.6 1.5 %combine.1 = f32[64,1536]{1,0:T(8,128)} custom-call(s32[1]{0:T(128)} %bitcast.core_ref, bf16[64,1536]{1,0:T(8,128)(2,1)S(1)} %get-tuple-element.37.keep_ref, bf16[64,1536]{1,0:T(8,128)(2,1)S(1)} %collective-permute-done.11.got_ref, s32[1536]{0:T(1024)S(1)} %copy-done), custom_call_target="tpu_custom_call" | custom-call | tf_op jit(solution)/shard_map/combine/pallas_call | solution.py:301
Async XLA Ops:
  0.0 2.1 %collective-permute-start = (bf16[2,64,1536]{2,1,0:T(8,128)(2,1)}, bf16[2,64,1536]{2,1,0:T(8,128)(2,1)S(1)}, u32[]{:S(2)}, u32[]{:S(2)}) collective-permute-start(bf16[2,64,1536]{2,1,0:T(8,128)(2,1)} %refs_0_.3), channel_id=1, source_target_pairs={{0,1},{1,0},{2,3},{3,2},{4,5},{5,4},{6,7},{7,6},{8,9},{9,8},{10,11... | collective-permute-start | bytes 1179656 | tf_op jit(solution)/shard_map/ppermute | solution.py:25
  0.5 1.6 %collective-permute-start.1 = (s32[2,64]{1,0:T(2,128)}, s32[2,64]{1,0:T(2,128)S(1)}, u32[]{:S(2)}, u32[]{:S(2)}) collective-permute-start(s32[2,64]{1,0:T(2,128)} %refs_2_.2), channel_id=1, source_target_pairs={{0,1},{1,0},{2,3},{3,2},{4,5},{5,4},{6,7},{7,6},{8,9},{9,8},{10,11... | collective-permute-start | bytes 1544 | tf_op jit(solution)/shard_map/ppermute | solution.py:25
  2.6 11.9 %collective-permute-start.2 = (bf16[64,1536]{1,0:T(8,128)(2,1)S(1)}, bf16[64,1536]{1,0:T(8,128)(2,1)S(1)}, u32[]{:S(2)}, u32[]{:S(2)}) collective-permute-start(bf16[64,1536]{1,0:T(8,128)(2,1)S(1)} %get-tuple-element.26), channel_id=1, source_target_pairs={{0,14},{1,15},{2,12},{3,13},{4,10},{5,11},{6,8},{7,9},{8,6},{9,7},... | collective-permute-start | bytes 589832 | tf_op jit(solution)/shard_map/ppermute | solution.py:25
  8.6 12.7 %collective-permute-start.4 = (bf16[128,384]{1,0:T(8,128)(2,1)S(1)}, bf16[128,384]{1,0:T(8,128)(2,1)S(1)}, u32[]{:S(2)}, u32[]{:S(2)}) collective-permute-start(bf16[128,384]{1,0:T(8,128)(2,1)S(1)} %get-tuple-element.27.refs_2_.refs_0_), channel_id=1, source_target_pairs={{0,8},{1,9},{2,10},{3,11},{4,12},{5,13},{6,14},{7,15},{8,0},{9,1},... | collective-permute-start | bytes 294920 | tf_op jit(solution)/shard_map/ppermute | solution.py:25
  8.6 13.5 %collective-permute-start.9 = (bf16[128,384]{1,0:T(8,128)(2,1)S(1)}, bf16[128,384]{1,0:T(8,128)(2,1)S(1)}, u32[]{:S(2)}, u32[]{:S(2)}) collective-permute-start(bf16[128,384]{1,0:T(8,128)(2,1)S(1)} %get-tuple-element.27.refs_2_.refs_0_), channel_id=1, source_target_pairs={{0,4},{1,5},{2,6},{3,7},{4,0},{5,1},{6,2},{7,3},{8,12},{9,13},{10,... | collective-permute-start | bytes 294920 | tf_op jit(solution)/shard_map/ppermute | solution.py:25
  14.5 17.1 %collective-permute-start.3 = (bf16[64,1536]{1,0:T(8,128)(2,1)S(1)}, bf16[64,1536]{1,0:T(8,128)(2,1)S(1)}, u32[]{:S(2)}, u32[]{:S(2)}) collective-permute-start(bf16[64,1536]{1,0:T(8,128)(2,1)S(1)} %collective-permute-done.2.mirrored_ref), channel_id=1, source_target_pairs={{0,1},{1,0},{2,3},{3,2},{4,5},{5,4},{6,7},{7,6},{8,9},{9,8},{10,11... | collective-permute-start | bytes 589832 | tf_op jit(solution)/shard_map/ppermute | solution.py:25
  21.3 4.6 %collective-permute-start.6 = (bf16[128,384]{1,0:T(8,128)(2,1)S(1)}, bf16[128,384]{1,0:T(8,128)(2,1)S(1)}, u32[]{:S(2)}, u32[]{:S(2)}) collective-permute-start(bf16[128,384]{1,0:T(8,128)(2,1)S(1)} %collective-permute-done.4.refs_4_), channel_id=1, source_target_pairs={{0,4},{1,5},{2,6},{3,7},{4,0},{5,1},{6,2},{7,3},{8,12},{9,13},{10,... | collective-permute-start | bytes 294920 | tf_op jit(solution)/shard_map/ppermute | solution.py:25
  21.3 9.9 %collective-permute-start.8 = (bf16[128,384]{1,0:T(8,128)(2,1)S(1)}, bf16[128,384]{1,0:T(8,128)(2,1)S(1)}, u32[]{:S(2)}, u32[]{:S(2)}) collective-permute-start(bf16[128,384]{1,0:T(8,128)(2,1)S(1)} %get-tuple-element.27.refs_2_.refs_0_), channel_id=1, source_target_pairs={{0,2},{1,3},{2,0},{3,1},{4,6},{5,7},{6,4},{7,5},{8,10},{9,11},{10,... | collective-permute-start | bytes 294920 | tf_op jit(solution)/shard_map/ppermute | solution.py:25
  22.1 9.1 %collective-permute-start.10 = (bf16[128,384]{1,0:T(8,128)(2,1)S(1)}, bf16[128,384]{1,0:T(8,128)(2,1)S(1)}, u32[]{:S(2)}, u32[]{:S(2)}) collective-permute-start(bf16[128,384]{1,0:T(8,128)(2,1)S(1)} %collective-permute-done.9.refs_2_), channel_id=1, source_target_pairs={{0,2},{1,3},{2,0},{3,1},{4,6},{5,7},{6,4},{7,5},{8,10},{9,11},{10,... | collective-permute-start | bytes 294920 | tf_op jit(solution)/shard_map/ppermute | solution.py:25
  23.3 9.0 %collective-permute-start.5 = (bf16[128,384]{1,0:T(8,128)(2,1)S(1)}, bf16[128,384]{1,0:T(8,128)(2,1)S(1)}, u32[]{:S(2)}, u32[]{:S(2)}) collective-permute-start(bf16[128,384]{1,0:T(8,128)(2,1)S(1)} %collective-permute-done.4.refs_4_), channel_id=1, source_target_pairs={{0,2},{1,3},{2,0},{3,1},{4,6},{5,7},{6,4},{7,5},{8,10},{9,11},{10,... | collective-permute-start | bytes 294920 | tf_op jit(solution)/shard_map/ppermute | solution.py:25
  25.9 6.4 %collective-permute-start.7 = (bf16[128,384]{1,0:T(8,128)(2,1)S(1)}, bf16[128,384]{1,0:T(8,128)(2,1)S(1)}, u32[]{:S(2)}, u32[]{:S(2)}) collective-permute-start(bf16[128,384]{1,0:T(8,128)(2,1)S(1)} %collective-permute-done.6.refs_5_), channel_id=1, source_target_pairs={{0,2},{1,3},{2,0},{3,1},{4,6},{5,7},{6,4},{7,5},{8,10},{9,11},{10,... | collective-permute-start | bytes 294920 | tf_op jit(solution)/shard_map/ppermute | solution.py:25
  32.3 4.2 %copy-start = (s32[1536]{0:T(1024)S(1)}, s32[1536]{0:T(1024)}, u32[]{:S(2)}) copy-start(s32[1536]{0:T(1024)} %perm_ref.1) | copy-start | bytes 18436
  35.1 1.5 %collective-permute-start.11 = (bf16[64,1536]{1,0:T(8,128)(2,1)S(1)}, bf16[64,1536]{1,0:T(8,128)(2,1)S(1)}, u32[]{:S(2)}, u32[]{:S(2)}) collective-permute-start(bf16[64,1536]{1,0:T(8,128)(2,1)S(1)} %get-tuple-element.38), channel_id=1, source_target_pairs={{0,1},{1,0},{2,3},{3,2},{4,5},{5,4},{6,7},{7,6},{8,9},{9,8},{10,11... | collective-permute-start | bytes 589832 | tf_op jit(solution)/shard_map/ppermute | solution.py:25
